TPU v7x, 128 devices: a whole 4x4x4 slice. The times are simulated.
128 devices in a mesh: pipe: 2 (over y_lo), ctx: 16 (over y_hi, x, core), tp: 4 (over z).
Axes of the slice: x: 4, y: 4 (y_hi: 2, y_lo: 2; y = y_hi * 2 + y_lo), z: 4, core: 2. Of those that a mesh axis runs over, the one named last changes fastest.
Arguments:
- queries: bfloat16 [2, 8192, 4096], P('pipe', 'ctx', 'tp'), may hold values from -24 to 24
- keys: bfloat16 [2, 8192, 4096], P('pipe', 'ctx', 'tp'), may hold values from -24 to 24
- values: bfloat16 [2, 8192, 4096], P('pipe', 'ctx', 'tp'), may hold values from -6 to 6
- stream: bfloat16 [2, 8192, 8192], P('pipe', 'ctx', 'tp'), may hold values from -6 to 6
- grad_stream: bfloat16 [2, 8192, 8192], P('pipe', 'ctx', 'tp'), may hold values from -6 to 6
- out_proj: bfloat16 [2, 4096, 8192], P('pipe', 'tp'), may hold values from -0.09375 to 0.09375
- doc_ids: int32 [2, 8192], P('pipe'), may hold values from 0 to 7, never falling along the last dimension, each value on 1 to 1536 neighbouring positions
Outputs:
- grad_queries: bfloat16 [2, 8192, 4096], P('pipe', 'ctx', 'tp')
- grad_keys: bfloat16 [2, 8192, 4096], P('pipe', 'ctx', 'tp')
- grad_values: bfloat16 [2, 8192, 4096], P('pipe', 'ctx', 'tp')
- next_stream: bfloat16 [2, 8192, 8192], P('pipe', 'ctx', 'tp')
- next_grad: bfloat16 [2, 8192, 8192], P('pipe', 'ctx', 'tp')
Inputs may be any that keep to these rules, and one draw needn't show every extreme that they name: `doc_ids`: document numbers never fall along a micro-batch; a document has at most 1536 tokens.
All inputs are finite; a program needn't handle non-finite values.
Results may differ from a plain program's by a relative error of at most 0.02.
Values may be sent and summed in bfloat16 or wider, within the bound.
A program may use at most 192 MiB of HBM per device.

v0:
```python
import jax
import jax.numpy as jnp
from jax import lax
from jax.sharding import PartitionSpec as P

HD = 128
WINDOW = 512


NEG = -1e30


def from_behind(block, axis, distance):
    devices = range(lax.axis_size(axis))
    route = [(i - distance, i) for i in devices if i - distance in devices]
    return lax.ppermute(block, axis, route)


def shifted(block, axis, distance):
    devices = range(lax.axis_size(axis))
    route = [((i - distance) % len(devices), i) for i in devices]
    return lax.ppermute(block, axis, route)


def block_terms(query_block, key_block, value_block, dout_block, visible):
    scaling = HD ** (-0.5)
    scores = (
        jnp.einsum("qhd,khd->hqk", query_block, key_block, preferred_element_type=jnp.float32)
        * scaling
    )
    masked = jnp.where(visible[None], scores, NEG)
    row_max = jnp.max(masked, axis=-1, keepdims=True)
    exponent = jnp.where(visible[None], jnp.exp(masked - row_max), 0.0)
    row_sum = jnp.sum(exponent, axis=-1, keepdims=True)
    probability = exponent / row_sum
    weights = probability.astype(jnp.bfloat16)
    attended = jnp.einsum(
        "hqk,khd->qhd", weights, value_block, preferred_element_type=jnp.float32
    ).astype(jnp.bfloat16)
    row_delta = jnp.einsum("qhd,qhd->hq", dout_block, attended, preferred_element_type=jnp.float32)[
        ..., None
    ]
    d_prob = jnp.einsum("qhd,khd->hqk", dout_block, value_block, preferred_element_type=jnp.float32)
    d_score = (probability * (d_prob - row_delta)).astype(jnp.bfloat16)
    d_value = jnp.einsum("hqk,qhd->khd", weights, dout_block, preferred_element_type=jnp.float32)
    d_query = (
        jnp.einsum("hqk,khd->qhd", d_score, key_block, preferred_element_type=jnp.float32) * scaling
    ).astype(jnp.bfloat16)
    d_key = (
        jnp.einsum("hqk,qhd->khd", d_score, query_block, preferred_element_type=jnp.float32)
        * scaling
    )
    return (attended, d_query, d_key, d_value)


def body(queries, keys, values, stream, grad_stream, out_proj, doc_ids):
    row_count = queries.shape[1]
    feature = queries.shape[2]
    head_count = feature // HD
    weight = out_proj[0]
    grad_rows = grad_stream[0]
    d_out = lax.dot_general(
        lax.all_gather(grad_rows, "tp", axis=1, tiled=True),
        weight,
        (((1,), (1,)), ((), ())),
        preferred_element_type=jnp.float32,
    ).astype(jnp.bfloat16)
    pair_own = jnp.stack([keys[0], values[0]])
    pair_prev = from_behind(pair_own, "ctx", 1)
    key_all = jnp.concatenate([pair_prev[0], keys[0]], 0).reshape(2 * row_count, head_count, HD)
    value_all = jnp.concatenate([pair_prev[1], values[0]], 0).reshape(2 * row_count, head_count, HD)
    shard_index = lax.axis_index("ctx")
    query_pos = shard_index * row_count + jnp.arange(row_count, dtype=jnp.int32)
    key_pos = (shard_index - 1) * row_count + jnp.arange(2 * row_count, dtype=jnp.int32)
    doc_row = doc_ids[0]
    query_doc = lax.dynamic_slice_in_dim(doc_row, shard_index * row_count, row_count)
    prev_doc = lax.dynamic_slice_in_dim(
        doc_row, jnp.maximum(shard_index - 1, 0) * row_count, row_count
    )
    key_doc = jnp.concatenate([prev_doc, query_doc], 0)
    visible = (key_pos[None, :] <= query_pos[:, None]) & (
        query_pos[:, None] - key_pos[None, :] < WINDOW
    )
    visible = visible & (key_pos[None, :] >= 0) & (key_doc[None, :] == query_doc[:, None])
    query_block = queries[0].reshape(row_count, head_count, HD)
    dout_block = d_out.reshape(row_count, head_count, HD)
    attended, d_query, d_key, d_value = block_terms(
        query_block, key_all, value_all, dout_block, visible
    )
    earlier_terms = jnp.stack(
        [
            d_key[:row_count].reshape(row_count, feature),
            d_value[:row_count].reshape(row_count, feature),
        ]
    )
    returned = from_behind(earlier_terms.astype(jnp.bfloat16), "ctx", -1).astype(
        earlier_terms.dtype
    )
    key_total = d_key[row_count:].reshape(row_count, feature) + returned[0]
    value_total = d_value[row_count:].reshape(row_count, feature) + returned[1]
    attended_flat = attended.reshape(row_count, feature)
    partial_value = jnp.dot(attended_flat, weight, preferred_element_type=jnp.float32).astype(
        jnp.bfloat16
    )
    own_share = lax.psum_scatter(partial_value, "tp", scatter_dimension=1, tiled=True).astype(
        jnp.float32
    )
    rebuilt = (stream[0].astype(jnp.float32) - own_share).astype(jnp.bfloat16)
    paired = shifted(jnp.stack([rebuilt, grad_rows]), "pipe", -1)
    stream_next = paired[0][None]
    grad_next = paired[1][None]
    grad_queries = d_query.reshape(1, row_count, feature)
    grad_keys = key_total.astype(jnp.bfloat16).reshape(1, row_count, feature)
    grad_values = value_total.astype(jnp.bfloat16).reshape(1, row_count, feature)
    return (grad_queries, grad_keys, grad_values, stream_next, grad_next)


def solution(mesh):
    in_specs = (
        P("pipe", "ctx", "tp"),
        P("pipe", "ctx", "tp"),
        P("pipe", "ctx", "tp"),
        P("pipe", "ctx", "tp"),
        P("pipe", "ctx", "tp"),
        P("pipe", "tp", None),
        P("pipe", None),
    )
    out_specs = (
        P("pipe", "ctx", "tp"),
        P("pipe", "ctx", "tp"),
        P("pipe", "ctx", "tp"),
        P("pipe", "ctx", "tp"),
        P("pipe", "ctx", "tp"),
    )
    return jax.shard_map(body, mesh=mesh, in_specs=in_specs, out_specs=out_specs, check_vma=False)
```

profile of v0, /device:TPU:22, one launch (start us, length us, event | category | flops | bytes accessed | tf_op | source)
XLA Modules:
  0.0 351.0 jit_solution(7472228304027143302)
XLA Ops:
  11.5 1.9 collective-permute-start
  14.1 1.9 copy.65
  18.1 1.7 fusion.20
  19.8 19.4 %collective-permute-done = bf16[2,512,1024]{1,2,0:T(8,128)(2,1)} collective-permute-done((bf16[2,512,1024]{1,2,0:T(8,128)(2,1)}, bf16[2,512,1024]{1,2,0:T(8,128)(2,1)}, u32[]{:S(2)}, u32[]{:S(2)}) %collective-permute-start) | collective-permute-done | bytes 2097184 | tf_op jit(solution)/shard_map/ppermute | solution.py:16
  39.2 3.0 fusion.39
  43.8 2.6 copy.35
  46.5 8.1 %fusion.31 = f32[8,1024,512]{2,1,0:T(8,128)} fusion(bf16[512,8,128]{0,2,1:T(8,128)(2,1)S(1)} %bitcast.73, bf16[512,8,128]{2,0,1:T(8,128)(2,1)S(1)} %copy.32, bf16[512,8,128]{2,0,1:T(8,128)(2,1)S(1)} %copy.31), kind=kOutput, calls=%fused_computation.41 | convolution fusion | flops 1077936128 | bytes 19922944 | tf_op jit(solution)/shard_map/qhd,khd->hqk/dot_general | solution.py:28
  54.6 18.6 %fusion.40 = (f32[8,512]{1,0:T(8,128)S(1)}, f32[8,512,1024]{1,2,0:T(8,128)}) fusion(f32[8,1024,512]{2,1,0:T(8,128)} %fusion.31, pred[512,1024]{0,1:T(8,128)(4,1)} %fusion.20), kind=kOutput, calls=%fused_computation.57 | output fusion | flops 29361152 | bytes 34095104 | tf_op jit(solution)/shard_map/sub | solution.py:33
  73.2 9.4 %fusion.13 = bf16[8,512,1024]{1,2,0:T(8,128)(2,1)} fusion(f32[8,512,1024]{1,2,0:T(8,128)} %get-tuple-element.24, f32[8,512]{1,0:T(8,128)S(1)} %get-tuple-element.23), kind=kLoop, calls=%fused_computation.15 | loop fusion | flops 8388608 | bytes 25182208 | tf_op jit(solution)/shard_map/convert_element_type | solution.py:36
  82.6 12.5 %all-gather.3.cloned.1.call-done = bf16[1,512,8192]{2,1,0:T(8,128)(2,1)} async-done(((bf16[1,512,2048]{2,1,0:T(8,128)(2,1)}), bf16[1,512,8192]{2,1,0:T(8,128)(2,1)}) %all-gather.3.cloned.1.call-update) | async-done | bytes 8388624 | tf_op jit(solution)/shard_map/all_gather | solution.py:63
  95.1 14.8 %fusion.26 = bf16[64,8,8,128]{3,1,2,0:T(8,128)(2,1)S(1)} fusion(bf16[1,1024,8192]{2,1,0:T(8,128)(2,1)} %param.12, bf16[1,512,8192]{2,1,0:T(8,128)(2,1)} %all-gather.3.cloned.1.call-done), kind=kOutput, calls=%fused_computation.40 | convolution fusion | flops 8590458880 | bytes 26214400 | tf_op jit(solution)/shard_map/dot_general | solution.py:62
  112.7 1.9 copy.60
  114.7 5.5 %multiply_reduce_fusion = (f32[8,512]{1,0:T(8,128)S(1)}, bf16[8,128,512]{2,1,0:T(8,128)(2,1)S(1)}) fusion(f32[8,512,128]{1,2,0:T(8,128)S(1)} %copy.60, bf16[8,512,1024]{1,2,0:T(8,128)(2,1)} %fusion.13, bf16[512,8,128]{2,0,1:T(8,128)(2,1)} %copy.36, bf16[512,8,128]{2,0,1:T(8,128)(2,1)} %copy.35), kind=kOutput, calls=%fused_computation.32 | convolution fusion | flops 1080029184 | bytes 13647872 | tf_op jit(solution)/shard_map/hqk,khd->qhd/dot_general | solution.py:37
  120.1 16.9 %fusion.6 = bf16[512,8192]{1,0:T(8,128)(2,1)} fusion(bf16[512,1024]{0,1:T(8,128)(2,1)S(1)} %bitcast.84, bf16[1,1024,8192]{2,1,0:T(8,128)(2,1)} %param.12), kind=kOutput, calls=%fused_computation.9 | convolution fusion | flops 8594128896 | bytes 26214400 | tf_op jit(solution)/shard_map/dot_general | solution.py:102
  139.7 79.1 %reduce-scatter.2.cloned.1.call-done = bf16[512,2048]{1,0:T(8,128)(2,1)} async-done(((bf16[512,8192]{1,0:T(8,128)(2,1)}), bf16[512,2048]{1,0:T(8,128)(2,1)}) %reduce-scatter.2.cloned.1.call-update) | async-done | bytes 2097168 | tf_op jit(solution)/shard_map/reduce_scatter | solution.py:105
  218.8 3.0 fusion.15
  221.8 2.4 pad_maximum_fusion
  225.5 10.1 %multiply_convert_fusion = bf16[8,512,1024]{1,2,0:T(8,128)(2,1)} fusion(bf16[512,8,128]{0,2,1:T(8,128)(2,1)} %copy.45, f32[8,512]{1,0:T(8,128)S(1)} %get-tuple-element.25, f32[8,512,1024]{1,2,0:T(8,128)} %get-tuple-element.24, f32[8,512]{1,0:T(8,128)S(1)} %get-tuple-element.23, bf16[512,8,128]{2,0,1:T(8,128)(2,1)S(1)} %copy-done.10, ...), kind=kOutput, calls=%fused_computation.6 | convolution fusion | flops 1094713344 | bytes 28344320 | tf_op jit(solution)/shard_map/qhd,khd->hqk/dot_general | solution.py:43
  235.5 6.2 %multiply_bitcast_fusion = f32[1024,8,128]{0,2,1:T(8,128)S(1)} fusion(bf16[8,512,1024]{1,2,0:T(8,128)(2,1)} %multiply_convert_fusion, bf16[512,8,128]{0,2,1:T(8,128)(2,1)S(1)} %bitcast.74), kind=kOutput, calls=%fused_computation.19 | convolution fusion | flops 1074790400 | bytes 13631488 | tf_op jit(solution)/shard_map/hqk,qhd->khd/dot_general | solution.py:50
  241.8 2.0 copy-done.1
  245.0 6.2 %convolution_bitcast_fusion = f32[1024,8,128]{0,2,1:T(8,128)S(1)} fusion(bf16[512,8,128]{0,2,1:T(8,128)(2,1)S(1)} %copy-done.12, bf16[8,512,1024]{1,2,0:T(8,128)(2,1)} %fusion.13), kind=kOutput, calls=%fused_computation.20 | convolution fusion | flops 1073741824 | bytes 13631488 | tf_op jit(solution)/shard_map/hqk,qhd->khd/dot_general | solution.py:45
  251.2 1.9 copy-done
  255.3 2.0 collective-permute-start.1
  258.9 3.1 copy.49
  262.0 1.8 copy.50
  263.8 6.1 %multiply_convert_fusion.1 = bf16[8,128,512]{2,1,0:T(8,128)(2,1)} fusion(bf16[8,512,1024]{1,2,0:T(8,128)(2,1)} %multiply_convert_fusion, bf16[512,8,128]{2,0,1:T(8,128)(2,1)S(1)} %copy-done.9, bf16[512,8,128]{2,0,1:T(8,128)(2,1)} %copy-done.11), kind=kOutput, calls=%fused_computation.33 | convolution fusion | flops 1078984704 | bytes 11534336 | tf_op jit(solution)/shard_map/hqk,khd->qhd/dot_general | solution.py:47
  269.9 2.4 copy.51
  272.3 8.9 %collective-permute-done.1 = bf16[2,512,1024]{2,1,0:T(8,128)(2,1)} collective-permute-done((bf16[2,512,1024]{2,1,0:T(8,128)(2,1)}, bf16[2,512,1024]{2,1,0:T(8,128)(2,1)}, u32[]{:S(2)}, u32[]{:S(2)}) %collective-permute-start.1) | collective-permute-done | bytes 2097184 | tf_op jit(solution)/shard_map/ppermute | solution.py:16
  281.2 2.0 convert_element_type.55
  283.3 2.0 fusion.16
  285.3 54.0 %collective-permute-done.2 = bf16[2,512,2048]{2,1,0:T(8,128)(2,1)} collective-permute-done((bf16[2,512,2048]{2,1,0:T(8,128)(2,1)}, bf16[2,512,2048]{2,1,0:T(8,128)(2,1)}, u32[]{:S(2)}, u32[]{:S(2)}) %collective-permute-start.2) | collective-permute-done | bytes 4194336 | tf_op jit(solution)/shard_map/ppermute | solution.py:22
  339.3 4.8 %fusion.38 = (bf16[1,512,2048]{2,1,0:T(8,128)(2,1)}, bf16[1,512,2048]{2,1,0:T(8,128)(2,1)}) fusion(bf16[2,512,2048]{2,1,0:T(8,128)(2,1)} %collective-permute-done.2), kind=kLoop, calls=%fused_computation.55 | loop fusion | bytes 8388608 | tf_op jit(solution)/shard_map/slice | solution.py:111
  (52 shorter events, 20.2 us)
Async XLA Ops:
  7.2 2.3 copy-start.13
  7.2 87.9 %all-gather.3.cloned.1.call-start = ((), (), s32[]{:S(2)}) async-start(), calls=%async_computation.2 | async-start | bytes 10485760 | tf_op jit(solution)/shard_map/all_gather | solution.py:63
  7.9 210.9 %reduce-scatter.2.cloned.1.call-start = ((), (), s32[]{:S(2)}) async-start(), calls=%async_computation.1 | async-start | bytes 10485760 | tf_op jit(solution)/shard_map/reduce_scatter | solution.py:105
  11.5 27.7 %collective-permute-start = (bf16[2,512,1024]{1,2,0:T(8,128)(2,1)}, bf16[2,512,1024]{1,2,0:T(8,128)(2,1)}, u32[]{:S(2)}, u32[]{:S(2)}) collective-permute-start(bf16[2,512,1024]{1,2,0:T(8,128)(2,1)} %pad_maximum_fusion.1), channel_id=1, source_target_pairs={{0,4},{4,8},{8,12},{12,16},{16,20},{20,24},{24,28},{28,32},{32,36}... | collective-permute-start | bytes 6291464 | tf_op jit(solution)/shard_map/ppermute | solution.py:16
  14.1 32.4 %copy-start.8 = (bf16[512,8,128]{2,0,1:T(8,128)(2,1)}, bf16[512,8,128]{2,0,1:T(8,128)(2,1)S(1)}, u32[]{:S(2)}) copy-start(bf16[512,8,128]{2,0,1:T(8,128)(2,1)S(1)} %copy.32) | copy-start | bytes 3145732
  43.8 10.7 %copy-start.11 = (bf16[512,8,128]{2,0,1:T(8,128)(2,1)}, bf16[512,8,128]{2,0,1:T(8,128)(2,1)S(1)}, u32[]{:S(2)}) copy-start(bf16[512,8,128]{2,0,1:T(8,128)(2,1)S(1)} %copy.31) | copy-start | bytes 3145732
  110.2 1.0 copy-start.3
  137.1 1.2 copy-start.4
  139.7 82.1 %copy-start.7 = (bf16[1,512,2048]{2,1,0:T(8,128)(2,1)S(1)}, bf16[1,512,2048]{2,1,0:T(8,128)(2,1)}, u32[]{:S(2)}) copy-start(bf16[1,512,2048]{2,1,0:T(8,128)(2,1)} %param.11) | copy-start | bytes 6291460
  221.8 3.6 %copy-start.10 = (bf16[512,8,128]{2,0,1:T(8,128)(2,1)S(1)}, bf16[512,8,128]{2,0,1:T(8,128)(2,1)}, u32[]{:S(2)}) copy-start(bf16[512,8,128]{2,0,1:T(8,128)(2,1)} %copy.36) | copy-start | bytes 3145732
  224.3 115.0 %collective-permute-start.2 = (bf16[2,512,2048]{2,1,0:T(8,128)(2,1)}, bf16[2,512,2048]{2,1,0:T(8,128)(2,1)}, u32[]{:S(2)}, u32[]{:S(2)}) collective-permute-start(bf16[2,512,2048]{2,1,0:T(8,128)(2,1)} %pad_maximum_fusion), channel_id=1, source_target_pairs={{64,0},{0,64},{65,1},{1,65},{66,2},{2,66},{67,3},{3,67},{68,4},{4,... | collective-permute-start | bytes 12582920 | tf_op jit(solution)/shard_map/ppermute | solution.py:22
  241.8 2.0 copy-start.1
  243.7 1.2 copy-start.12
  251.2 1.9 copy-start
  253.8 3.6 %copy-start.2 = (f32[1024,8,128]{0,2,1:T(8,128)S(1)}, f32[1024,8,128]{0,2,1:T(8,128)}, u32[]{:S(2)}) copy-start(f32[1024,8,128]{0,2,1:T(8,128)} %copy-done.1) | copy-start | bytes 12582916
  255.3 25.9 %collective-permute-start.1 = (bf16[2,512,1024]{2,1,0:T(8,128)(2,1)}, bf16[2,512,1024]{2,1,0:T(8,128)(2,1)}, u32[]{:S(2)}, u32[]{:S(2)}) collective-permute-start(bf16[2,512,1024]{2,1,0:T(8,128)(2,1)} %pad_maximum_fusion.4), channel_id=1, source_target_pairs={{4,0},{8,4},{12,8},{16,12},{20,16},{24,20},{28,24},{32,28},{36,32}... | collective-permute-start | bytes 6291464 | tf_op jit(solution)/shard_map/ppermute | solution.py:16
  258.9 3.1 slice-start
  258.9 4.9 %copy-start.9 = (bf16[512,8,128]{2,0,1:T(8,128)(2,1)S(1)}, bf16[512,8,128]{2,0,1:T(8,128)(2,1)}, u32[]{:S(2)}) copy-start(bf16[512,8,128]{2,0,1:T(8,128)(2,1)} %copy-done.8) | copy-start | bytes 3145732
  269.9 13.4 %copy-start.5 = (f32[1,512,1024]{2,1,0:T(8,128)S(1)}, f32[1,512,1024]{2,1,0:T(8,128)}, u32[]{:S(2)}) copy-start(f32[1,512,1024]{2,1,0:T(8,128)} %copy.49) | copy-start | bytes 6291460
  272.3 11.0 %copy-start.6 = (f32[1,512,1024]{2,1,0:T(8,128)S(1)}, f32[1,512,1024]{2,1,0:T(8,128)}, u32[]{:S(2)}) copy-start(f32[1,512,1024]{2,1,0:T(8,128)} %copy.50) | copy-start | bytes 6291460
Sparse Core Ops, SparseCore 0:
  9.6 85.4 all-gather.2
  137.2 81.5 reduce-scatter.1
where the time goes:
time: 352 us; the launch traced here: 351 us
  waiting for transfers between devices  175 us (50%)
  matrix products  73.9 us (21%)
  other arithmetic  43.7 us (12%)
  local copies, waits for them, and re-layouts  39.1 us (11%)
  between operations  14.3 us (4%)
  starting transfers between devices  5.21 us (1%)
    reduce_scatter x1, waiting for transfers between devices, body(): lax.psum_scatter(partial_value, 'tp', scatter_dimension=1, tiled=True)  79.1 us
    ppermute x1, waiting for transfers between devices, shifted(): return lax.ppermute(block, axis, route)  54 us
    ppermute x2, waiting for transfers between devices, from_behind(): return lax.ppermute(block, axis, route)  28.4 us
    sub x1, other arithmetic, block_terms(): exponent = jnp.where(visible[None], jnp.exp(masked - row_max), 0.0)  18.6 us
    dot_general x1, matrix products, body(): jnp.dot(attended_flat, weight, preferred_element_type=jnp.float32)  16.9 us
    dot_general x1, matrix products, body(): lax.dot_general(lax.all_gather(grad_rows, 'tp', axis=1, tiled=True), weig...  14.8 us
    unnamed x33, local copies, waits for them, and re-layouts  13.3 us
    all_gather x1, waiting for transfers between devices, body(): lax.all_gather(grad_rows, 'tp', axis=1, tiled=True)  12.5 us
  transfers between devices with their start and end apart: 5, of which 5 were waited for; matrix products, arithmetic and copies ran while one was open for 28% of the time, Pallas kernels for 0%

commit v1 on v0

v1 whole, which is shorter than its diff:
```python
import functools
import math

import jax
import jax.numpy as jnp
from jax import lax
from jax.experimental import pallas as pl
from jax.experimental.pallas import tpu as pltpu
from jax.sharding import PartitionSpec as P

HD = 128
WINDOW = 512
NEG = -1e30
MESH = pl.DeviceIdType.MESH
NT = (((1,), (1,)), ((), ()))
OWN, LEFT, RIGHT, FAR = 0, 1, 2, 3


def dot(a, b, dims=(((1,), (0,)), ((), ()))):
    return lax.dot_general(a, b, dims, preferred_element_type=jnp.float32)


def kernel(
    rows, width, shard, ctx_n, tp_n, pipe_n,
    q_hbm, k_hbm, v_hbm, s_hbm, g_hbm, w_hbm, doc_ref,
    dq_hbm, dk_hbm, dv_hbm, ns_hbm, ng_hbm,
    w_s, gat, q_s, k_s, v_s, st_s, acc, dot_s, att, bias,
    acck, accv, ret_out, ret_in, dq_s, fin, in_a, in_b, fin_l, fin_r,
    lsem, osem, ags, agr, fws, fwr, hs, hr, rts, rtr, rss, rsr, pgs, pgr, prs, prr,
):
    pipe = lax.axis_index("pipe")
    c = lax.axis_index("ctx")
    z = lax.axis_index("tp")
    right, left = lax.rem(z + 1, tp_n), lax.rem(z + tp_n - 1, tp_n)
    nxt, prv = lax.rem(c + 1, ctx_n), lax.rem(c + ctx_n - 1, ctx_n)
    other = lax.rem(pipe + 1, pipe_n)
    has_prev, has_next = c > 0, c < ctx_n - 1
    qb, sub, half = rows // 2, rows // 4, shard // 2
    kw = 3 * qb
    heads = width // HD

    barrier = pltpu.get_barrier_semaphore()
    for where in ({"tp": right}, {"tp": left}, {"ctx": nxt}, {"ctx": prv}, {"pipe": other}):
        pl.semaphore_signal(barrier, inc=1, device_id=where, device_id_type=MESH)

    def local(src, dst, sem):
        return pltpu.make_async_copy(src, dst, sem)

    shards = (z, left, right, lax.rem(z + 2, tp_n))
    loads = {}
    for rel in (OWN, LEFT, RIGHT, FAR):
        cols = pl.ds(pl.multiple_of(shards[rel] * shard, shard), shard)
        loads[rel] = local(w_hbm.at[0, :, cols], w_s.at[rel], lsem.at[rel])
    loads["g"] = local(g_hbm.at[0], gat.at[OWN], lsem.at[4])
    loads["q"] = local(q_hbm.at[0], q_s, lsem.at[5])
    loads["k"] = local(k_hbm.at[0], k_s.at[pl.ds(rows, rows)], lsem.at[6])
    loads["v"] = local(v_hbm.at[0], v_s.at[pl.ds(rows, rows)], lsem.at[7])
    loads["s"] = local(s_hbm.at[0], st_s, lsem.at[8])

    def remote(src, dst, ssem, rsem, where):
        return pltpu.make_async_remote_copy(
            src_ref=src, dst_ref=dst, send_sem=ssem, recv_sem=rsem,
            device_id=where, device_id_type=MESH,
        )

    to_right, to_left = {"tp": right}, {"tp": left}

    def piece(s):
        return pl.ds(s * sub, sub)

    lo, hi = pl.ds(0, half), pl.ds(half, half)

    def own(s):
        src = g_hbm.at[0, piece(s)]
        return (
            remote(src, gat.at[LEFT, piece(s)], ags.at[0, s], agr.at[0, s], to_right),
            remote(src, gat.at[RIGHT, piece(s)], ags.at[1, s], agr.at[1, s], to_left),
        )

    def passed(s):
        return (
            remote(gat.at[LEFT, piece(s), lo], gat.at[FAR, piece(s), lo], fws.at[0, s], fwr.at[0, s], to_right),
            remote(gat.at[RIGHT, piece(s), hi], gat.at[FAR, piece(s), hi], fws.at[1, s], fwr.at[1, s], to_left),
        )

    def halo():
        return (
            remote(k_hbm.at[0], k_s.at[pl.ds(0, rows)], hs.at[0], hr.at[0], {"ctx": nxt}),
            remote(v_hbm.at[0], v_s.at[pl.ds(0, rows)], hs.at[1], hr.at[1], {"ctx": nxt}),
        )

    def back(t):
        part = pl.ds(t * qb, qb)
        return tuple(
            remote(ret_out.at[i, part], ret_in.at[i, part], rts.at[i, t], rtr.at[i, t], {"ctx": prv})
            for i in range(2)
        )

    def far_terms(s):
        return (
            remote(gat.at[FAR, piece(s), lo], in_a.at[piece(s)], rss.at[0, 0, s], rsr.at[0, 0, s], to_right),
            remote(gat.at[FAR, piece(s), hi], in_b.at[piece(s)], rss.at[0, 1, s], rsr.at[0, 1, s], to_left),
        )

    def plain_terms(s):
        return (
            remote(gat.at[RIGHT, piece(s), hi], fin_l.at[piece(s), hi], rss.at[1, 0, s], rsr.at[1, 0, s], to_right),
            remote(gat.at[LEFT, piece(s), lo], fin_r.at[piece(s), lo], rss.at[1, 1, s], rsr.at[1, 1, s], to_left),
        )

    def merged_terms(s):
        return (
            remote(gat.at[RIGHT, piece(s), lo], fin_l.at[piece(s), lo], rss.at[2, 0, s], rsr.at[2, 0, s], to_right),
            remote(gat.at[LEFT, piece(s), hi], fin_r.at[piece(s), hi], rss.at[2, 1, s], rsr.at[2, 1, s], to_left),
        )

    def grad_on(s):
        return remote(g_hbm.at[0, piece(s)], ng_hbm.at[0, piece(s)], pgs.at[s], pgr.at[s], {"pipe": other})

    def stream_on(s):
        return remote(st_s.at[piece(s)], ns_hbm.at[0, piece(s)], prs.at[s], prr.at[s], {"pipe": other})

    def start(copies):
        for copy in copies:
            copy.start()

    def arrive(copies):
        for copy in copies:
            copy.wait_recv()

    def sent(copies):
        for copy in copies:
            copy.wait_send()

    loads["g"].start()
    for key in (OWN, "q", "k", "v", LEFT, RIGHT, FAR, "s"):
        loads[key].start()

    pl.semaphore_wait(barrier, 5)
    start(own(0))

    @pl.when(has_next)
    def _():
        start(halo())

    start(own(1))

    @pl.when(jnp.logical_not(has_prev))
    def _():
        k_s[pl.ds(0, rows), :] = jnp.zeros((rows, width), k_s.dtype)
        v_s[pl.ds(0, rows), :] = jnp.zeros((rows, width), v_s.dtype)

    @pl.when(jnp.logical_not(has_next))
    def _():
        ret_in[...] = jnp.zeros(ret_in.shape, ret_in.dtype)

    own_doc = doc_ref[:, pl.ds(pl.multiple_of(c * rows, rows), rows)].astype(jnp.float32)
    old_doc = doc_ref[:, pl.ds(pl.multiple_of(jnp.maximum(c - 1, 0) * rows, rows), rows)].astype(jnp.float32)
    key_row = jnp.concatenate([old_doc, own_doc], axis=1)
    key_doc = jnp.transpose(jnp.broadcast_to(key_row, (HD, 2 * rows)))
    a = lax.broadcasted_iota(jnp.int32, (kw, qb), 0)
    b = lax.broadcasted_iota(jnp.int32, (kw, qb), 1)
    for t in range(2):
        seen = (a <= b + rows) & (a > b + (rows - WINDOW))
        seen = seen & ((a + t * qb >= rows) | has_prev)
        columns = jnp.broadcast_to(key_doc[t * qb:t * qb + kw, :1], (kw, qb))
        seen = seen & (columns == own_doc[:, t * qb:(t + 1) * qb])
        bias[t] = jnp.where(seen, 0.0, NEG)

    kstep = min(512, shard)

    def d_out_term(t, rel, first):
        def step(i, _):
            cols = pl.ds(pl.multiple_of(i * kstep, kstep), kstep)
            term = dot(w_s[rel, :, cols], gat[rel, pl.ds(t * qb, qb), cols], NT)
            if first:
                @pl.when(i == 0)
                def _():
                    acc[...] = term

                @pl.when(i > 0)
                def _():
                    acc[...] += term
            else:
                acc[...] += term
            return 0

        lax.fori_loop(0, shard // kstep, step, 0)

    def d_out_store(t):
        dot_s[:, pl.ds(t * qb, qb)] = acc[...].astype(jnp.bfloat16)

    scaling = HD ** -0.5

    def head(h, t):
        cols = pl.ds(pl.multiple_of(h * HD, HD), HD)
        keys = k_s[pl.ds(t * qb, kw), cols]
        values = v_s[pl.ds(t * qb, kw), cols]
        queries = q_s[pl.ds(t * qb, qb), cols]
        d_out = dot_s[cols, pl.ds(t * qb, qb)]
        scores = dot(keys, queries, NT) + bias[t]
        top = jnp.max(scores, axis=0, keepdims=True)
        exponent = jnp.exp2((scores - top) * (scaling * math.log2(math.e)))
        total = jnp.sum(exponent, axis=0, keepdims=True)
        probs = exponent * (1.0 / total)
        weights = probs.astype(jnp.bfloat16)
        out = dot(jnp.transpose(values), weights)
        att[pl.ds(t * qb, qb), cols] = jnp.transpose(out).astype(jnp.bfloat16)
        out = out.astype(jnp.bfloat16).astype(jnp.float32)
        delta = jnp.sum(d_out.astype(jnp.float32) * out, axis=0, keepdims=True)
        d_prob = dot(values, d_out)
        d_score = (probs * (d_prob - delta)).astype(jnp.bfloat16)
        d_value = dot(weights, d_out, NT)
        d_key = dot(d_score, queries) * scaling
        d_query = dot(jnp.transpose(keys), d_score) * scaling
        dq_s[pl.ds(t * qb, qb), cols] = jnp.transpose(d_query).astype(jnp.bfloat16)
        for i, (total_ref, term) in enumerate(((acck, d_key), (accv, d_value))):
            if t == 0:
                ret_out[i, pl.ds(0, qb), cols] = term[:qb].astype(jnp.bfloat16)
                total_ref[pl.ds(0, 2 * qb), cols] = term[qb:]
            else:
                ret_out[i, pl.ds(qb, qb), cols] = (total_ref[pl.ds(0, qb), cols] + term[:qb]).astype(jnp.bfloat16)
                total_ref[pl.ds(qb, qb), cols] += term[qb:2 * qb]
                total_ref[pl.ds(2 * qb, qb), cols] = term[2 * qb:]

    def attention(t, hooks):
        def step(i, _):
            for at, hook in hooks.items():
                @pl.when(i == at)
                def _():
                    hook()
            for j in range(2):
                head(i * 2 + j, t)
            return 0

        lax.fori_loop(0, heads // 2, step, 0)

    nstep = min(512, shard)

    def partial(t, rel):
        def step(i, _):
            cols = pl.ds(pl.multiple_of(i * nstep, nstep), nstep)
            term = dot(att[pl.ds(t * qb, qb), :], w_s[rel, :, cols])
            gat[rel, pl.ds(t * qb, qb), cols] = term.astype(jnp.bfloat16)
            return 0

        lax.fori_loop(0, shard // nstep, step, 0)

    def pass_on(s):
        arrive(own(s))
        start(passed(s))

    def merge(s):
        arrive(far_terms(s))
        gat[RIGHT, piece(s), lo] = (
            gat[RIGHT, piece(s), lo].astype(jnp.float32) + in_a[piece(s), :].astype(jnp.float32)
        ).astype(jnp.bfloat16)
        gat[LEFT, piece(s), hi] = (
            gat[LEFT, piece(s), hi].astype(jnp.float32) + in_b[piece(s), :].astype(jnp.float32)
        ).astype(jnp.bfloat16)
        start(merged_terms(s))

    def finish(s):
        arrive(plain_terms(s))
        arrive(merged_terms(s))
        branch = (
            gat[OWN, piece(s), :].astype(jnp.float32)
            + fin_l[piece(s), :].astype(jnp.float32)
            + fin_r[piece(s), :].astype(jnp.float32)
        )
        st_s[piece(s), :] = (st_s[piece(s), :].astype(jnp.float32) - branch).astype(jnp.bfloat16)
        stream_on(s).start()

    loads[OWN].wait()
    loads["g"].wait()
    d_out_term(0, OWN, True)
    for key in (LEFT, RIGHT, FAR, "q", "k", "v"):
        loads[key].wait()
    pass_on(0)
    pass_on(1)
    start(own(2))
    start(own(3))
    d_out_term(0, LEFT, False)
    d_out_term(0, RIGHT, False)

    @pl.when(has_prev)
    def _():
        arrive(halo())

    for s in range(4):
        grad_on(s).start()
    arrive(passed(0))
    arrive(passed(1))
    d_out_term(0, FAR, False)
    d_out_store(0)

    last = heads // 2 - 1
    attention(0, {min(2, last): lambda: pass_on(2)})
    pass_on(3)

    @pl.when(has_prev)
    def _():
        start(back(0))

    out_q0 = local(dq_s.at[pl.ds(0, qb)], dq_hbm.at[0, pl.ds(0, qb)], osem.at[0])
    out_q0.start()
    sent(passed(0))
    sent(passed(1))
    partial(0, FAR)
    partial(0, RIGHT)
    start(far_terms(0))
    start(far_terms(1))
    partial(0, LEFT)
    start(plain_terms(0))
    start(plain_terms(1))
    partial(0, OWN)

    d_out_term(1, OWN, True)
    d_out_term(1, LEFT, False)
    d_out_term(1, RIGHT, False)
    arrive(passed(2))
    arrive(passed(3))
    d_out_term(1, FAR, False)
    d_out_store(1)
    attention(1, {min(2, last): lambda: merge(0), min(3, last): lambda: merge(1)} if last > 2 else {})
    if last <= 2:
        merge(0)
        merge(1)

    @pl.when(has_prev)
    def _():
        start(back(1))

    out_q1 = local(dq_s.at[pl.ds(qb, qb)], dq_hbm.at[0, pl.ds(qb, qb)], osem.at[1])
    out_q1.start()
    sent(passed(2))
    sent(passed(3))
    partial(1, FAR)
    partial(1, RIGHT)
    start(far_terms(2))
    start(far_terms(3))
    partial(1, LEFT)
    start(plain_terms(2))
    start(plain_terms(3))
    partial(1, OWN)
    loads["s"].wait()
    finish(0)
    finish(1)
    merge(2)
    merge(3)

    @pl.when(has_next)
    def _():
        arrive(back(0))
        arrive(back(1))

    outs = []
    for i, (total_ref, ref) in enumerate(((acck, dk_hbm), (accv, dv_hbm))):
        fin[i] = (total_ref[pl.ds(qb, rows), :] + ret_in[i].astype(jnp.float32)).astype(jnp.bfloat16)
        outs.append(local(fin.at[i], ref.at[0], osem.at[2 + i]))
        outs[-1].start()
    finish(2)
    finish(3)

    for s in range(4):
        sent(own(s))
        sent(far_terms(s))
        sent(plain_terms(s))
        sent(merged_terms(s))
        grad_on(s).wait_send()
        grad_on(s).wait_recv()
        stream_on(s).wait_send()
        stream_on(s).wait_recv()

    @pl.when(has_next)
    def _():
        sent(halo())

    @pl.when(has_prev)
    def _():
        sent(back(0))
        sent(back(1))

    for copy in (out_q0, out_q1, *outs):
        copy.wait()


def body(queries, keys, values, stream, grad_stream, out_proj, doc_ids):
    rows, width = queries.shape[1], queries.shape[2]
    shard = stream.shape[2]
    bf, f32 = jnp.bfloat16, jnp.float32
    qb = rows // 2
    dma = pltpu.SemaphoreType.DMA
    hbm = pl.BlockSpec(memory_space=pl.ANY)
    sizes = (lax.axis_size("ctx"), lax.axis_size("tp"), lax.axis_size("pipe"))
    assert sizes[1] == 4 and rows == WINDOW
    like = lambda x: jax.ShapeDtypeStruct(x.shape, x.dtype)
    return pl.pallas_call(
        functools.partial(kernel, rows, width, shard, *sizes),
        out_shape=(like(queries), like(keys), like(values), like(stream), like(grad_stream)),
        in_specs=[hbm] * 6 + [pl.BlockSpec(memory_space=pltpu.VMEM)],
        out_specs=(hbm,) * 5,
        scratch_shapes=[
            pltpu.VMEM((4, width, shard), bf),
            pltpu.VMEM((4, rows, shard), bf),
            pltpu.VMEM((rows, width), bf),
            pltpu.VMEM((2 * rows, width), bf),
            pltpu.VMEM((2 * rows, width), bf),
            pltpu.VMEM((rows, shard), bf),
            pltpu.VMEM((width, qb), f32),
            pltpu.VMEM((width, rows), bf),
            pltpu.VMEM((rows, width), bf),
            pltpu.VMEM((2, 3 * qb, qb), f32),
            pltpu.VMEM((3 * qb, width), f32),
            pltpu.VMEM((3 * qb, width), f32),
            pltpu.VMEM((2, rows, width), bf),
            pltpu.VMEM((2, rows, width), bf),
            pltpu.VMEM((rows, width), bf),
            pltpu.VMEM((2, rows, width), bf),
            pltpu.VMEM((rows, shard // 2), bf),
            pltpu.VMEM((rows, shard // 2), bf),
            pltpu.VMEM((rows, shard), bf),
            pltpu.VMEM((rows, shard), bf),
            dma((9,)), dma((4,)),
            dma((2, 4)), dma((2, 4)), dma((2, 4)), dma((2, 4)),
            dma((2,)), dma((2,)), dma((2, 2)), dma((2, 2)),
            dma((3, 2, 4)), dma((3, 2, 4)),
            dma((4,)), dma((4,)), dma((4,)), dma((4,)),
        ],
        compiler_params=pltpu.CompilerParams(
            collective_id=0, has_side_effects=True, vmem_limit_bytes=67043328
        ),
    )(queries, keys, values, stream, grad_stream, out_proj, doc_ids)


def solution(mesh):
    spec = P("pipe", "ctx", "tp")
    in_specs = (spec,) * 5 + (P("pipe", "tp", None), P("pipe", None))
    return jax.shard_map(body, mesh=mesh, in_specs=in_specs, out_specs=(spec,) * 5, check_vma=False)
```

time: 352 us -> 172 us (0.49)
  waiting for transfers between devices: 175 us -> 0 us
  Pallas kernels: 0 us -> 162 us
  matrix products: 73.9 us -> 0 us
  other arithmetic: 43.7 us -> 0 us
  local copies, waits for them, and re-layouts: 39.1 us -> 8.1 us
  between operations: 14.3 us -> 0.66 us
  starting transfers between devices: 5.21 us -> 0 us
    pallas_call x0 -> x1, Pallas kernels: none -> 162 us  [body(): pl.pallas_call(functools.partial(kernel, rows, width, shard, *sizes), out...]
    ppermute x3 -> x0, waiting for transfers between devices: 82.4 us -> none  [the longest x1 54 us: shifted(): return lax.ppermute(block, axis, route)]
    reduce_scatter x1 -> x0, waiting for transfers between devices: 79.1 us -> none  [body(): lax.psum_scatter(partial_value, 'tp', scatter_dimension=1, tiled=True)]
    dot_general x8 -> x0, matrix products: 73.9 us -> none  [the longest x1 16.9 us: body(): jnp.dot(attended_flat, weight, preferred_element_type=jnp.float32)]
    sub x1 -> x0, other arithmetic: 18.6 us -> none  [block_terms(): exponent = jnp.where(visible[None], jnp.exp(masked - row_max), 0.0)]
    convert_element_type x3 -> x0, other arithmetic: 13.4 us -> none  [the longest x1 9.41 us: block_terms(): weights = probability.astype(jnp.bfloat16)]
    all_gather x1 -> x0, waiting for transfers between devices: 12.5 us -> none  [body(): lax.all_gather(grad_rows, 'tp', axis=1, tiled=True)]
    slice x7 -> x0, local copies, waits for them, and re-layouts: 9.65 us -> none  [the longest x1 4.82 us: body(): grad_next = paired[1][None]]
  transfers between devices with their start and end apart: 5 -> 0, of which waited for: 5 -> 0; matrix products, arithmetic and copies ran while one was open for 28% -> 0% of each run, Pallas kernels for 0% -> 0%
where the time goes in v1:
time: 172 us; the launch traced here: 171 us
  Pallas kernels  162 us (94%)
  local copies, waits for them, and re-layouts  8.1 us (5%)
    pallas_call x1, Pallas kernels, body(): pl.pallas_call(functools.partial(kernel, rows, width, shard, *sizes), out...  162 us
    unnamed x13, local copies, waits for them, and re-layouts  8.1 us

profile of v1, /device:TPU:22, one launch (start us, length us, event | category | flops | bytes accessed | tf_op | source)
XLA Modules:
  0.0 171.2 jit_solution(2579028168354706171)
XLA Ops:
  0.6 162.4 %shard_map.110 = (bf16[1,512,1024]{2,1,0:T(8,128)(2,1)}, bf16[1,512,1024]{2,1,0:T(8,128)(2,1)}, bf16[1,512,1024]{2,1,0:T(8,128)(2,1)}, bf16[1,512,2048]{2,1,0:T(8,128)(2,1)}, bf16[1,512,2048]{2,1,0:T(8,128)(2,1)}) custom-call(bf16[1,512,1024]{2,1,0:T(8,128)(2,1)} %q_hbm.1, bf16[1,512,1024]{2,1,0:T(8,128)(2,1)} %k_hbm.1, bf16[1,512,1024]{2,1,0:T(8,128)(2,1)} %v_hbm.1, ...), custom_call_target="tpu_custom_call" | custom-call | tf_op jit(solution)/shard_map/pallas_call | solution.py:398
  163.0 0.0 copy-start.3
  163.1 0.0 copy-start.2
  163.1 2.4 %copy.17 = bf16[1,512,1024]{2,1,0:T(8,128)(2,1)} copy(bf16[1,512,1024]{2,1,0:T(8,128)(2,1)} %get-tuple-element.10) | data formatting | bytes 2097152
  165.5 0.0 copy-done.3
  165.5 0.0 copy-start.1
  165.5 1.0 copy.18
  166.5 0.0 copy-done.2
  166.5 1.0 copy.19
  167.4 0.1 copy-done.1
  167.5 0.0 copy-start
  167.5 1.3 copy.20
  168.8 1.0 copy-done
  169.8 1.3 copy.21
Async XLA Ops:
  163.0 2.4 %copy-start.3 = (bf16[1,512,1024]{2,1,0:T(8,128)(2,1)S(1)}, bf16[1,512,1024]{2,1,0:T(8,128)(2,1)}, u32[]{:S(2)}) copy-start(bf16[1,512,1024]{2,1,0:T(8,128)(2,1)} %get-tuple-element.11) | copy-start | bytes 3145732
  163.1 3.4 %copy-start.2 = (bf16[1,512,1024]{2,1,0:T(8,128)(2,1)S(1)}, bf16[1,512,1024]{2,1,0:T(8,128)(2,1)}, u32[]{:S(2)}) copy-start(bf16[1,512,1024]{2,1,0:T(8,128)(2,1)} %get-tuple-element.12) | copy-start | bytes 3145732
  165.5 2.0 %copy-start.1 = (bf16[1,512,2048]{2,1,0:T(8,128)(2,1)S(1)}, bf16[1,512,2048]{2,1,0:T(8,128)(2,1)}, u32[]{:S(2)}) copy-start(bf16[1,512,2048]{2,1,0:T(8,128)(2,1)} %get-tuple-element.13) | copy-start | bytes 6291460
  167.5 2.3 %copy-start = (bf16[1,512,2048]{2,1,0:T(8,128)(2,1)S(1)}, bf16[1,512,2048]{2,1,0:T(8,128)(2,1)}, u32[]{:S(2)}) copy-start(bf16[1,512,2048]{2,1,0:T(8,128)(2,1)} %get-tuple-element.14) | copy-start | bytes 6291460

commit v2 on v0

v2 whole, which is shorter than its diff:
```python
import functools
import math

import jax
import jax.numpy as jnp
from jax import lax
from jax.experimental import pallas as pl
from jax.experimental.pallas import tpu as pltpu
from jax.sharding import PartitionSpec as P

HD = 128
WINDOW = 512
NEG = -1e30
MESH = pl.DeviceIdType.MESH
NT = (((1,), (1,)), ((), ()))
OWN, RIGHT, FAR, LEFT = 0, 1, 2, 3
PAIRS = 4


def dot(a, b, dims=(((1,), (0,)), ((), ()))):
    return lax.dot_general(a, b, dims, preferred_element_type=jnp.float32)


def kernel(
    rows, width, shard, ctx_n, tp_n, pipe_n,
    q_hbm, k_hbm, v_hbm, s_hbm, g_hbm, w_hbm, doc_ref,
    dq_hbm, dk_hbm, dv_hbm, ns_hbm, ng_hbm,
    w_s, g_s, q_s, k_s, v_s, st_s, part, att, out_t, prob, bias,
    acc, ret_out, ret_in, mine, dq_s, in_a, in_b, fin_l, fin_r,
    lsem, osem, w1s, w1r, wxs, wxr, wcs, wcr, ats, atr, hs, hr, rts, rtr, rss, rsr, pgs, pgr, prs, prr,
):
    pipe = lax.axis_index("pipe")
    c = lax.axis_index("ctx")
    z = lax.axis_index("tp")
    nxt, prv = lax.rem(c + 1, ctx_n), lax.rem(c + ctx_n - 1, ctx_n)
    other = lax.rem(pipe + 1, pipe_n)
    has_prev, has_next = c > 0, c < ctx_n - 1
    qb, sub = rows // 2, rows // 4
    kw, pw = 3 * qb, 2 * HD
    row = c // 8
    x, core = lax.rem(c, 8) // 2, lax.rem(c, 2)
    mate = 1 - core
    xs = (x, lax.rem(x + 1, 4), lax.rem(x + 3, 4), lax.rem(x + 2, 4))

    def at_x(chip, side):
        return {"ctx": row * 8 + chip * 2 + side}

    to_z = {d: {"tp": lax.rem(z + d, tp_n)} for d in (RIGHT, FAR, LEFT)}
    x_up, x_down, x_mate = at_x(xs[1], core), at_x(xs[2], core), at_x(x, mate)

    barrier = pltpu.get_barrier_semaphore()
    partners = (*to_z.values(), x_up, x_down, x_mate, {"ctx": nxt}, {"ctx": prv}, {"pipe": other})
    for where in partners:
        pl.semaphore_signal(barrier, inc=1, device_id=where, device_id_type=MESH)

    def local(src, dst, sem):
        return pltpu.make_async_copy(src, dst, sem)

    def remote(src, dst, ssem, rsem, where):
        return pltpu.make_async_remote_copy(
            src_ref=src, dst_ref=dst, send_sem=ssem, recv_sem=rsem,
            device_id=where, device_id_type=MESH,
        )

    def features(d):
        return pl.ds(pl.multiple_of(lax.rem(z + d, tp_n) * shard, shard), shard)

    def block(chip, side):
        return pl.ds(pl.multiple_of((chip * 2 + side) * HD, HD), HD)

    def pair_rows(o):
        return pl.ds(pl.multiple_of(xs[o] * pw, pw), pw)

    loads = {
        "q": local(q_hbm.at[0], q_s, lsem.at[0]),
        "k": local(k_hbm.at[0], k_s.at[pl.ds(rows, rows)], lsem.at[1]),
        "v": local(v_hbm.at[0], v_s.at[pl.ds(rows, rows)], lsem.at[2]),
        "g": local(g_hbm.at[0], g_s, lsem.at[3]),
        "w": local(w_hbm.at[0, :, features(OWN)], w_s.at[OWN], lsem.at[4]),
        "s": local(s_hbm.at[0], st_s, lsem.at[5]),
    }

    def w_first(d):
        there = (4 - d) % 4
        here = block(x, core)
        return remote(w_hbm.at[0, here, features(d)], w_s.at[there, here], w1s.at[there - 1], w1r.at[there - 1], to_z[d])

    def w_piece(r, chip, side, ssem, rsem, where):
        here = w_s.at[r, block(chip, side)]
        return remote(here, here, ssem, rsem, where)

    def w_up(r, chip):
        return w_piece(r, chip, core, wxs.at[0, r - 1], wxr.at[0, r - 1], x_up)

    def w_down(r, chip):
        return w_piece(r, chip, core, wxs.at[1, r - 1], wxr.at[1, r - 1], x_down)

    def w_far(r, chip):
        return w_piece(r, chip, core, wxs.at[2, r - 1], wxr.at[2, r - 1], x_up if r == FAR else x_down)

    def w_mate(r, o, side):
        return w_piece(r, xs[o], side, wcs.at[o, r - 1], wcr.at[o, r - 1], x_mate)

    def own_block(r):
        w_first((4 - r) % 4).wait_recv()
        w_up(r, x).start()
        w_down(r, x).start()
        w_mate(r, 0, core).start()

    def up_block(r):
        w_down(r, xs[1]).wait_recv()
        if r != FAR:
            w_far(r, xs[1]).start()
        w_mate(r, 1, core).start()

    def down_block(r):
        w_up(r, xs[2]).wait_recv()
        if r == FAR:
            w_far(r, xs[2]).start()
        w_mate(r, 2, core).start()

    def far_block(r):
        w_far(r, xs[3]).wait_recv()
        w_mate(r, 3, core).start()

    def mate_blocks(o):
        for r in (LEFT, RIGHT, FAR):
            w_mate(r, o, mate).wait_recv()

    lo, hi = pl.ds(0, qb), pl.ds(qb, qb)

    def att_own(o):
        return (
            remote(att.at[OWN, o], att.at[LEFT, o], ats.at[0, o], atr.at[0, o], to_z[RIGHT]),
            remote(att.at[OWN, o], att.at[RIGHT, o], ats.at[1, o], atr.at[1, o], to_z[LEFT]),
        )

    def att_pass(o):
        return (
            remote(att.at[LEFT, o, lo], att.at[FAR, o, lo], ats.at[2, o], atr.at[2, o], to_z[RIGHT]),
            remote(att.at[RIGHT, o, hi], att.at[FAR, o, hi], ats.at[3, o], atr.at[3, o], to_z[LEFT]),
        )

    def far_terms(o):
        return (
            remote(part.at[o, FAR, :, lo], in_a.at[o], rss.at[0, 0, o], rsr.at[0, 0, o], to_z[RIGHT]),
            remote(part.at[o, FAR, :, hi], in_b.at[o], rss.at[0, 1, o], rsr.at[0, 1, o], to_z[LEFT]),
        )

    def plain_terms(o):
        return (
            remote(part.at[o, RIGHT, :, hi], fin_l.at[o, :, hi], rss.at[1, 0, o], rsr.at[1, 0, o], to_z[RIGHT]),
            remote(part.at[o, LEFT, :, lo], fin_r.at[o, :, lo], rss.at[1, 1, o], rsr.at[1, 1, o], to_z[LEFT]),
        )

    def merged_terms(o):
        return (
            remote(part.at[o, RIGHT, :, lo], fin_l.at[o, :, lo], rss.at[2, 0, o], rsr.at[2, 0, o], to_z[RIGHT]),
            remote(part.at[o, LEFT, :, hi], fin_r.at[o, :, hi], rss.at[2, 1, o], rsr.at[2, 1, o], to_z[LEFT]),
        )

    def halo():
        return (
            remote(k_hbm.at[0], k_s.at[pl.ds(0, rows)], hs.at[0], hr.at[0], {"ctx": nxt}),
            remote(v_hbm.at[0], v_s.at[pl.ds(0, rows)], hs.at[1], hr.at[1], {"ctx": nxt}),
        )

    def back(p):
        return tuple(
            remote(ret_out.at[i, p], ret_in.at[i, p], rts.at[i, p], rtr.at[i, p], {"ctx": prv})
            for i in range(2)
        )

    def grad_on(s):
        here = pl.ds(s * sub, sub)
        return remote(g_hbm.at[0, here], ng_hbm.at[0, here], pgs.at[s], pgr.at[s], {"pipe": other})

    wide = shard // 4

    def stream_on(n):
        cols = pl.ds(n * wide, wide)
        return remote(st_s.at[:, cols], ns_hbm.at[0, :, cols], prs.at[n], prr.at[n], {"pipe": other})

    def start(copies):
        for copy in copies:
            copy.start()

    def arrive(copies):
        for copy in copies:
            copy.wait_recv()

    def sent(copies):
        for copy in copies:
            copy.wait_send()

    def fill_bias():
        own_doc = doc_ref[:, pl.ds(pl.multiple_of(c * rows, rows), rows)].astype(jnp.float32)
        old_doc = doc_ref[:, pl.ds(pl.multiple_of(jnp.maximum(c - 1, 0) * rows, rows), rows)].astype(jnp.float32)
        key_doc = jnp.transpose(jnp.broadcast_to(jnp.concatenate([old_doc, own_doc], axis=1), (HD, 2 * rows)))
        a = lax.broadcasted_iota(jnp.int32, (kw, qb), 0)
        b = lax.broadcasted_iota(jnp.int32, (kw, qb), 1)
        for t in range(2):
            seen = (a <= b + rows) & (a > b + (rows - WINDOW))
            seen = seen & ((a + t * qb >= rows) | has_prev)
            columns = jnp.broadcast_to(key_doc[t * qb:t * qb + kw, :1], (kw, qb))
            seen = seen & (columns == own_doc[:, t * qb:(t + 1) * qb])
            bias[t] = jnp.where(seen, 0.0, NEG)

    scaling = HD ** -0.5

    def forward(o):
        def step(i, _):
            cols = pl.ds(pl.multiple_of(xs[o] * pw + i * HD, HD), HD)
            mine_cols = pl.ds(pl.multiple_of(i * HD, HD), HD)
            for t in range(2):
                tokens = pl.ds(t * qb, qb)
                keys = k_s[pl.ds(t * qb, kw), cols]
                values = v_s[pl.ds(t * qb, kw), cols]
                scores = dot(keys, q_s[tokens, cols], NT) + bias[t]
                top = jnp.max(scores, axis=0, keepdims=True)
                exponent = jnp.exp2((scores - top) * (scaling * math.log2(math.e)))
                total = jnp.sum(exponent, axis=0, keepdims=True)
                weights = (exponent * (1.0 / total)).astype(jnp.bfloat16)
                prob[o * 2 + i, t] = weights
                out = dot(jnp.transpose(values), weights)
                out_t[o, mine_cols, tokens] = out.astype(jnp.bfloat16)
                att[OWN, o, tokens, mine_cols] = jnp.transpose(out).astype(jnp.bfloat16)
            return 0

        lax.fori_loop(0, 2, step, 0)

    def d_out_terms(o):
        def step(r, _):
            term = dot(w_s[r, pair_rows(o), :], g_s[...], NT)
            part[o, r] = term.astype(jnp.bfloat16)
            return 0

        lax.fori_loop(0, 4, step, 0)

    def add_into(r, o, cols, extra):
        part[o, r, :, cols] = (
            part[o, r, :, cols].astype(jnp.float32) + extra.astype(jnp.float32)
        ).astype(jnp.bfloat16)

    def merge(o):
        arrive(far_terms(o))
        add_into(RIGHT, o, lo, in_a[o])
        add_into(LEFT, o, hi, in_b[o])
        start(merged_terms(o))

    def d_out_done(o):
        arrive(plain_terms(o))
        arrive(merged_terms(o))
        total = part[o, OWN].astype(jnp.float32) + fin_l[o].astype(jnp.float32) + fin_r[o].astype(jnp.float32)
        part[o, OWN] = total.astype(jnp.bfloat16)

    def backward(o):
        def step(i, _):
            cols = pl.ds(pl.multiple_of(xs[o] * pw + i * HD, HD), HD)
            mine_cols = pl.ds(pl.multiple_of(i * HD, HD), HD)
            d_keys, d_values = [], []
            for t in range(2):
                tokens = pl.ds(t * qb, qb)
                keys = k_s[pl.ds(t * qb, kw), cols]
                values = v_s[pl.ds(t * qb, kw), cols]
                queries = q_s[tokens, cols]
                d_out = part[o, OWN, mine_cols, tokens]
                weights = prob[o * 2 + i, t]
                delta = jnp.sum(
                    d_out.astype(jnp.float32) * out_t[o, mine_cols, tokens].astype(jnp.float32),
                    axis=0, keepdims=True,
                )
                d_prob = dot(values, d_out)
                d_score = (weights.astype(jnp.float32) * (d_prob - delta)).astype(jnp.bfloat16)
                d_values.append(dot(weights, d_out, NT))
                d_keys.append(dot(d_score, queries) * scaling)
                d_query = dot(jnp.transpose(keys), d_score) * scaling
                dq_s[tokens, cols] = jnp.transpose(d_query).astype(jnp.bfloat16)
            for n, (early, late) in enumerate((d_keys, d_values)):
                ret_out[n, xs[o], pl.ds(0, qb), mine_cols] = early[:qb].astype(jnp.bfloat16)
                ret_out[n, xs[o], pl.ds(qb, qb), mine_cols] = (early[qb:2 * qb] + late[:qb]).astype(jnp.bfloat16)
                mine[n, o, pl.ds(0, qb), mine_cols] = early[2 * qb:] + late[qb:2 * qb]
                mine[n, o, pl.ds(qb, qb), mine_cols] = late[2 * qb:]
            return 0

        lax.fori_loop(0, 2, step, 0)

        @pl.when(has_prev)
        def _():
            start(back(xs[o]))

    def branch_term(o, cols):
        left = jnp.concatenate([att[r, o] for r in range(4)], axis=1)
        return dot(left, w_s[:, pair_rows(o), cols].reshape(4 * pw, wide))

    def branch(o):
        def step(n, _):
            cols = pl.ds(pl.multiple_of(n * wide, wide), wide)
            term = branch_term(o, cols)
            acc[:, cols] = term if o == 0 else acc[:, cols] + term
            return 0

        lax.fori_loop(0, 4, step, 0)

    def rebuild(n):
        cols = pl.ds(n * wide, wide)
        total = acc[:, cols] + branch_term(3, cols)
        st_s[:, cols] = (st_s[:, cols].astype(jnp.float32) - total).astype(jnp.bfloat16)

    def att_relay(o):
        arrive(att_own(o))
        start(att_pass(o))

    for key in ("k", "v", "q", "w", "g", "s"):
        loads[key].start()

    pl.semaphore_wait(barrier, len(partners))
    w_first(RIGHT).start()
    w_first(LEFT).start()

    @pl.when(has_next)
    def _():
        start(halo())

    w_first(FAR).start()

    @pl.when(jnp.logical_not(has_prev))
    def _():
        k_s[pl.ds(0, rows), :] = jnp.zeros((rows, width), k_s.dtype)
        v_s[pl.ds(0, rows), :] = jnp.zeros((rows, width), v_s.dtype)

    @pl.when(jnp.logical_not(has_next))
    def _():
        ret_in[...] = jnp.zeros(ret_in.shape, ret_in.dtype)

    fill_bias()
    for key in ("k", "v", "q"):
        loads[key].wait()
    own_block(LEFT)
    own_block(RIGHT)
    own_block(FAR)

    @pl.when(has_prev)
    def _():
        arrive(halo())

    for s in range(4):
        grad_on(s).start()
    forward(0)
    start(att_own(0))
    up_block(LEFT)
    loads["w"].wait()
    loads["g"].wait()
    mate_blocks(0)
    d_out_terms(0)
    start(far_terms(0))
    start(plain_terms(0))
    forward(1)
    start(att_own(1))
    att_relay(0)
    merge(0)
    up_block(RIGHT)
    down_block(LEFT)
    forward(2)
    start(att_own(2))
    att_relay(1)
    forward(3)
    start(att_own(3))
    att_relay(2)
    d_out_done(0)
    down_block(RIGHT)
    up_block(FAR)
    arrive(att_pass(0))
    branch(0)
    att_relay(3)
    mate_blocks(1)
    d_out_terms(1)
    start(far_terms(1))
    start(plain_terms(1))
    backward(0)
    merge(1)
    far_block(LEFT)
    down_block(FAR)
    arrive(att_pass(1))
    branch(1)
    mate_blocks(2)
    d_out_terms(2)
    start(far_terms(2))
    start(plain_terms(2))
    arrive(att_pass(2))
    branch(2)
    far_block(RIGHT)
    far_block(FAR)
    arrive(att_pass(3))
    loads["s"].wait()
    mate_blocks(3)
    for n in range(4):
        rebuild(n)
        stream_on(n).start()
    d_out_terms(3)
    start(far_terms(3))
    start(plain_terms(3))
    merge(2)
    d_out_done(1)
    backward(1)
    merge(3)
    d_out_done(2)
    backward(2)
    d_out_done(3)
    backward(3)

    out_q = local(dq_s, dq_hbm.at[0], osem.at[0])
    out_q.start()
    outs = [out_q]

    @pl.when(has_next)
    def _():
        for p in range(PAIRS):
            arrive(back(p))

    for i, (ref, out) in enumerate(((k_s, dk_hbm), (v_s, dv_hbm))):
        here = ref.at[pl.ds(rows, rows)]
        for o in range(PAIRS):
            total = mine[i, o] + ret_in[i, xs[o]].astype(jnp.float32)
            ref[pl.ds(rows, rows), pair_rows(o)] = total.astype(jnp.bfloat16)
        outs.append(local(here, out.at[0], osem.at[1 + i]))
        outs[-1].start()

    for r in (LEFT, RIGHT, FAR):
        w_first((4 - r) % 4).wait_send()
        w_up(r, x).wait_send()
        w_down(r, x).wait_send()
        w_far(r, xs[1] if r != FAR else xs[2]).wait_send()
        for o in range(PAIRS):
            w_mate(r, o, core).wait_send()
    for o in range(PAIRS):
        sent(att_own(o))
        sent(att_pass(o))
        sent(far_terms(o))
        sent(plain_terms(o))
        sent(merged_terms(o))
        grad_on(o).wait_send()
        grad_on(o).wait_recv()
        stream_on(o).wait_send()
        stream_on(o).wait_recv()

    @pl.when(has_next)
    def _():
        sent(halo())

    @pl.when(has_prev)
    def _():
        for p in range(PAIRS):
            sent(back(p))

    for copy in outs:
        copy.wait()


def body(queries, keys, values, stream, grad_stream, out_proj, doc_ids):
    rows, width = queries.shape[1], queries.shape[2]
    shard = stream.shape[2]
    bf, f32 = jnp.bfloat16, jnp.float32
    qb, pw = rows // 2, 2 * HD
    dma = pltpu.SemaphoreType.DMA
    hbm = pl.BlockSpec(memory_space=pl.ANY)
    sizes = (lax.axis_size("ctx"), lax.axis_size("tp"), lax.axis_size("pipe"))
    assert sizes[0] % 8 == 0 and sizes[1] == 4 and rows == WINDOW and width == 8 * HD
    like = lambda x: jax.ShapeDtypeStruct(x.shape, x.dtype)
    return pl.pallas_call(
        functools.partial(kernel, rows, width, shard, *sizes),
        out_shape=(like(queries), like(keys), like(values), like(stream), like(grad_stream)),
        in_specs=[hbm] * 6 + [pl.BlockSpec(memory_space=pltpu.VMEM)],
        out_specs=(hbm,) * 5,
        scratch_shapes=[
            pltpu.VMEM((4, width, shard), bf),
            pltpu.VMEM((rows, shard), bf),
            pltpu.VMEM((rows, width), bf),
            pltpu.VMEM((2 * rows, width), bf),
            pltpu.VMEM((2 * rows, width), bf),
            pltpu.VMEM((rows, shard), bf),
            pltpu.VMEM((PAIRS, 4, pw, rows), bf),
            pltpu.VMEM((4, PAIRS, rows, pw), bf),
            pltpu.VMEM((PAIRS, pw, rows), bf),
            pltpu.VMEM((8, 2, 3 * qb, qb), bf),
            pltpu.VMEM((2, 3 * qb, qb), f32),
            pltpu.VMEM((rows, shard), f32),
            pltpu.VMEM((2, PAIRS, rows, pw), bf),
            pltpu.VMEM((2, PAIRS, rows, pw), bf),
            pltpu.VMEM((2, PAIRS, rows, pw), f32),
            pltpu.VMEM((rows, width), bf),
            pltpu.VMEM((PAIRS, pw, qb), bf),
            pltpu.VMEM((PAIRS, pw, qb), bf),
            pltpu.VMEM((PAIRS, pw, rows), bf),
            pltpu.VMEM((PAIRS, pw, rows), bf),
            dma((6,)), dma((3,)),
            dma((3,)), dma((3,)), dma((3, 3)), dma((3, 3)), dma((4, 3)), dma((4, 3)),
            dma((4, 4)), dma((4, 4)),
            dma((2,)), dma((2,)), dma((2, 4)), dma((2, 4)),
            dma((3, 2, 4)), dma((3, 2, 4)),
            dma((4,)), dma((4,)), dma((4,)), dma((4,)),
        ],
        compiler_params=pltpu.CompilerParams(
            collective_id=0, has_side_effects=True, vmem_limit_bytes=67043328
        ),
    )(queries, keys, values, stream, grad_stream, out_proj, doc_ids)


def solution(mesh):
    spec = P("pipe", "ctx", "tp")
    in_specs = (spec,) * 5 + (P("pipe", "tp", None), P("pipe", None))
    return jax.shard_map(body, mesh=mesh, in_specs=in_specs, out_specs=(spec,) * 5, check_vma=False)
```

time: 352 us -> 169 us (0.48)
  waiting for transfers between devices: 175 us -> 0 us
  Pallas kernels: 0 us -> 160 us
  matrix products: 73.9 us -> 0 us
  other arithmetic: 43.7 us -> 0 us
  local copies, waits for them, and re-layouts: 39.1 us -> 8.1 us
  between operations: 14.3 us -> 0.66 us
  starting transfers between devices: 5.21 us -> 0 us
    pallas_call x0 -> x1, Pallas kernels: none -> 160 us  [body(): pl.pallas_call(functools.partial(kernel, rows, width, shard, *sizes), out...]
    ppermute x3 -> x0, waiting for transfers between devices: 82.4 us -> none  [the longest x1 54 us: shifted(): return lax.ppermute(block, axis, route)]
    reduce_scatter x1 -> x0, waiting for transfers between devices: 79.1 us -> none  [body(): lax.psum_scatter(partial_value, 'tp', scatter_dimension=1, tiled=True)]
    dot_general x8 -> x0, matrix products: 73.9 us -> none  [the longest x1 16.9 us: body(): jnp.dot(attended_flat, weight, preferred_element_type=jnp.float32)]
    sub x1 -> x0, other arithmetic: 18.6 us -> none  [block_terms(): exponent = jnp.where(visible[None], jnp.exp(masked - row_max), 0.0)]
    convert_element_type x3 -> x0, other arithmetic: 13.4 us -> none  [the longest x1 9.41 us: block_terms(): weights = probability.astype(jnp.bfloat16)]
    all_gather x1 -> x0, waiting for transfers between devices: 12.5 us -> none  [body(): lax.all_gather(grad_rows, 'tp', axis=1, tiled=True)]
    slice x7 -> x0, local copies, waits for them, and re-layouts: 9.65 us -> none  [the longest x1 4.82 us: body(): grad_next = paired[1][None]]
  transfers between devices with their start and end apart: 5 -> 0, of which waited for: 5 -> 0; matrix products, arithmetic and copies ran while one was open for 28% -> 0% of each run, Pallas kernels for 0% -> 0%
where the time goes in v2:
time: 169 us
  Pallas kernels  160 us (95%)
  local copies, waits for them, and re-layouts  8.1 us (5%)
    pallas_call x1, Pallas kernels, body(): pl.pallas_call(functools.partial(kernel, rows, width, shard, *sizes), out...  160 us
    unnamed x13, local copies, waits for them, and re-layouts  8.1 us

profile of v2, /device:TPU:22, one launch (start us, length us, event | category | flops | bytes accessed | tf_op | source)
XLA Modules:
  0.0 168.7 jit_solution(5057892872855242967)
XLA Ops:
  0.6 159.9 %shard_map.110 = (bf16[1,512,1024]{2,1,0:T(8,128)(2,1)}, bf16[1,512,1024]{2,1,0:T(8,128)(2,1)}, bf16[1,512,1024]{2,1,0:T(8,128)(2,1)}, bf16[1,512,2048]{2,1,0:T(8,128)(2,1)}, bf16[1,512,2048]{2,1,0:T(8,128)(2,1)}) custom-call(bf16[1,512,1024]{2,1,0:T(8,128)(2,1)} %q_hbm.1, bf16[1,512,1024]{2,1,0:T(8,128)(2,1)} %k_hbm.1, bf16[1,512,1024]{2,1,0:T(8,128)(2,1)} %v_hbm.1, ...), custom_call_target="tpu_custom_call" | custom-call | tf_op jit(solution)/shard_map/pallas_call | solution.py:470
  160.5 0.0 copy-start.3
  160.6 0.0 copy-start.2
  160.6 2.4 %copy.17 = bf16[1,512,1024]{2,1,0:T(8,128)(2,1)} copy(bf16[1,512,1024]{2,1,0:T(8,128)(2,1)} %get-tuple-element.10) | data formatting | bytes 2097152
  163.0 0.0 copy-done.3
  163.0 0.0 copy-start.1
  163.0 1.0 copy.18
  163.9 0.0 copy-done.2
  164.0 1.0 copy.19
  164.9 0.1 copy-done.1
  165.0 0.0 copy-start
  165.0 1.3 copy.20
  166.3 1.0 copy-done
  167.3 1.3 copy.21
Async XLA Ops:
  160.5 2.4 %copy-start.3 = (bf16[1,512,1024]{2,1,0:T(8,128)(2,1)S(1)}, bf16[1,512,1024]{2,1,0:T(8,128)(2,1)}, u32[]{:S(2)}) copy-start(bf16[1,512,1024]{2,1,0:T(8,128)(2,1)} %get-tuple-element.11) | copy-start | bytes 3145732
  160.6 3.4 %copy-start.2 = (bf16[1,512,1024]{2,1,0:T(8,128)(2,1)S(1)}, bf16[1,512,1024]{2,1,0:T(8,128)(2,1)}, u32[]{:S(2)}) copy-start(bf16[1,512,1024]{2,1,0:T(8,128)(2,1)} %get-tuple-element.12) | copy-start | bytes 3145732
  163.0 2.0 %copy-start.1 = (bf16[1,512,2048]{2,1,0:T(8,128)(2,1)S(1)}, bf16[1,512,2048]{2,1,0:T(8,128)(2,1)}, u32[]{:S(2)}) copy-start(bf16[1,512,2048]{2,1,0:T(8,128)(2,1)} %get-tuple-element.13) | copy-start | bytes 6291460
  165.0 2.3 %copy-start = (bf16[1,512,2048]{2,1,0:T(8,128)(2,1)S(1)}, bf16[1,512,2048]{2,1,0:T(8,128)(2,1)}, u32[]{:S(2)}) copy-start(bf16[1,512,2048]{2,1,0:T(8,128)(2,1)} %get-tuple-element.14) | copy-start | bytes 6291460

commit v3 on v2

--- a/solution.py
+++ b/solution.py
@@ -26,8 +26,8 @@
     q_hbm, k_hbm, v_hbm, s_hbm, g_hbm, w_hbm, doc_ref,
     dq_hbm, dk_hbm, dv_hbm, ns_hbm, ng_hbm,
     w_s, g_s, q_s, k_s, v_s, st_s, part, att, out_t, prob, bias,
-    acc, ret_out, ret_in, mine, dq_s, in_a, in_b, fin_l, fin_r,
-    lsem, osem, w1s, w1r, wxs, wxr, wcs, wcr, ats, atr, hs, hr, rts, rtr, rss, rsr, pgs, pgr, prs, prr,
+    acc, ret_out, ret_in, relay, mine, dq_s, in_a, in_b, fin_l, fin_r,
+    lsem, osem, w1s, w1r, wxs, wxr, wcs, wcr, ats, atr, hs, hr, rts, rtr, rls, rlr, rss, rsr, pgs, pgr, prs, prr,
 ):
     pipe = lax.axis_index("pipe")
     c = lax.axis_index("ctx")
@@ -53,6 +53,22 @@
     for where in partners:
         pl.semaphore_signal(barrier, inc=1, device_id=where, device_id_type=MESH)
 
+    more_rows = c < ctx_n - 8
+    is_first = (lax.rem(c, 8) == 0) & has_prev
+    is_relay = (core == 0) & (x < 3) & more_rows
+    is_last = (lax.rem(c, 8) == 7) & more_rows
+    row_last = {"ctx": row * 8 + 7}
+    row_next = {"ctx": lax.rem(row * 8 + 8, ctx_n)}
+
+    @pl.when(is_relay)
+    def _():
+        pl.semaphore_signal(barrier, inc=1, device_id=row_next, device_id_type=MESH)
+
+    @pl.when(is_last)
+    def _():
+        for chip in range(3):
+            pl.semaphore_signal(barrier, inc=1, device_id=at_x(chip, 0), device_id_type=MESH)
+
     def local(src, dst, sem):
         return pltpu.make_async_copy(src, dst, sem)
 
@@ -80,52 +96,63 @@
         "s": local(s_hbm.at[0], st_s, lsem.at[5]),
     }
 
-    def w_first(d):
+    part_f = shard // 2
+
+    def w_first(d, f):
         there = (4 - d) % 4
         here = block(x, core)
-        return remote(w_hbm.at[0, here, features(d)], w_s.at[there, here], w1s.at[there - 1], w1r.at[there - 1], to_z[d])
-
-    def w_piece(r, chip, side, ssem, rsem, where):
-        here = w_s.at[r, block(chip, side)]
+        start_at = lax.rem(z + d, tp_n) * shard + f * part_f
+        cols = pl.ds(pl.multiple_of(start_at, part_f), part_f)
+        return remote(
+            w_hbm.at[0, here, cols], w_s.at[there, here, pl.ds(f * part_f, part_f)],
+            w1s.at[there - 1, f], w1r.at[there - 1, f], to_z[d],
+        )
+
+    def w_piece(r, f, chip, side, ssem, rsem, where):
+        here = w_s.at[r, block(chip, side), pl.ds(f * part_f, part_f)]
         return remote(here, here, ssem, rsem, where)
 
-    def w_up(r, chip):
-        return w_piece(r, chip, core, wxs.at[0, r - 1], wxr.at[0, r - 1], x_up)
-
-    def w_down(r, chip):
-        return w_piece(r, chip, core, wxs.at[1, r - 1], wxr.at[1, r - 1], x_down)
-
-    def w_far(r, chip):
-        return w_piece(r, chip, core, wxs.at[2, r - 1], wxr.at[2, r - 1], x_up if r == FAR else x_down)
-
-    def w_mate(r, o, side):
-        return w_piece(r, xs[o], side, wcs.at[o, r - 1], wcr.at[o, r - 1], x_mate)
-
-    def own_block(r):
-        w_first((4 - r) % 4).wait_recv()
-        w_up(r, x).start()
-        w_down(r, x).start()
-        w_mate(r, 0, core).start()
-
-    def up_block(r):
-        w_down(r, xs[1]).wait_recv()
-        if r != FAR:
-            w_far(r, xs[1]).start()
-        w_mate(r, 1, core).start()
-
-    def down_block(r):
-        w_up(r, xs[2]).wait_recv()
-        if r == FAR:
-            w_far(r, xs[2]).start()
-        w_mate(r, 2, core).start()
-
-    def far_block(r):
-        w_far(r, xs[3]).wait_recv()
-        w_mate(r, 3, core).start()
-
-    def mate_blocks(o):
-        for r in (LEFT, RIGHT, FAR):
-            w_mate(r, o, mate).wait_recv()
+    def w_up(r, f, chip):
+        return w_piece(r, f, chip, core, wxs.at[0, r - 1, f], wxr.at[0, r - 1, f], x_up)
+
+    def w_down(r, f, chip):
+        return w_piece(r, f, chip, core, wxs.at[1, r - 1, f], wxr.at[1, r - 1, f], x_down)
+
+    upward = ((RIGHT, 1), (FAR, 1))
+
+    def w_far(r, f, chip):
+        where = x_up if (r, f) in upward else x_down
+        return w_piece(r, f, chip, core, wxs.at[2, r - 1, f], wxr.at[2, r - 1, f], where)
+
+    def w_mate(r, f, o, side):
+        return w_piece(r, f, xs[o], side, wcs.at[o, r - 1, f], wcr.at[o, r - 1, f], x_mate)
+
+    def own_block(r, f):
+        w_first((4 - r) % 4, f).wait_recv()
+        w_up(r, f, x).start()
+        w_down(r, f, x).start()
+        w_mate(r, f, 0, core).start()
+
+    def up_block(r, f):
+        w_down(r, f, xs[1]).wait_recv()
+        if (r, f) not in upward:
+            w_far(r, f, xs[1]).start()
+        w_mate(r, f, 1, core).start()
+
+    def down_block(r, f):
+        w_up(r, f, xs[2]).wait_recv()
+        if (r, f) in upward:
+            w_far(r, f, xs[2]).start()
+        w_mate(r, f, 2, core).start()
+
+    def far_block(r, f):
+        w_far(r, f, xs[3]).wait_recv()
+        w_mate(r, f, 3, core).start()
+
+    def mate_blocks(o, halves=(0, 1)):
+        for f in halves:
+            for r in (LEFT, RIGHT, FAR):
+                w_mate(r, f, o, mate).wait_recv()
 
     lo, hi = pl.ds(0, qb), pl.ds(qb, qb)
 
@@ -170,6 +197,28 @@
             remote(ret_out.at[i, p], ret_in.at[i, p], rts.at[i, p], rtr.at[i, p], {"ctx": prv})
             for i in range(2)
         )
+
+    def to_relay(o):
+        where = {"ctx": jnp.maximum(row - 1, 0) * 8 + o * 2}
+        return tuple(
+            remote(ret_out.at[i, xs[o]], relay.at[i], rls.at[i, o], rlr.at[i], where)
+            for i in range(2)
+        )
+
+    def from_relay():
+        p = x + x // 2
+        return tuple(
+            remote(relay.at[i], ret_in.at[i, p], rts.at[i, 4], rtr.at[i, p], row_last)
+            for i in range(2)
+        )
+
+    def relay_on(chip):
+        @pl.when(is_relay & (x == chip))
+        def _():
+            arrive(tuple(
+                remote(ret_out.at[i, 0], relay.at[i], rls.at[i, 0], rlr.at[i], row_next) for i in range(2)
+            ))
+            start(from_relay())
 
     def grad_on(s):
         here = pl.ds(s * sub, sub)
@@ -279,33 +328,45 @@
             for n, (early, late) in enumerate((d_keys, d_values)):
                 ret_out[n, xs[o], pl.ds(0, qb), mine_cols] = early[:qb].astype(jnp.bfloat16)
                 ret_out[n, xs[o], pl.ds(qb, qb), mine_cols] = (early[qb:2 * qb] + late[:qb]).astype(jnp.bfloat16)
-                mine[n, o, pl.ds(0, qb), mine_cols] = early[2 * qb:] + late[qb:2 * qb]
-                mine[n, o, pl.ds(qb, qb), mine_cols] = late[2 * qb:]
+                mine[n, xs[o], pl.ds(0, qb), mine_cols] = early[2 * qb:] + late[qb:2 * qb]
+                mine[n, xs[o], pl.ds(qb, qb), mine_cols] = late[2 * qb:]
             return 0
 
         lax.fori_loop(0, 2, step, 0)
 
-        @pl.when(has_prev)
+        @pl.when(has_prev if o == 3 else has_prev & jnp.logical_not(is_first))
         def _():
             start(back(xs[o]))
 
-    def branch_term(o, cols):
-        left = jnp.concatenate([att[r, o] for r in range(4)], axis=1)
-        return dot(left, w_s[:, pair_rows(o), cols].reshape(4 * pw, wide))
-
-    def branch(o):
-        def step(n, _):
-            cols = pl.ds(pl.multiple_of(n * wide, wide), wide)
-            term = branch_term(o, cols)
-            acc[:, cols] = term if o == 0 else acc[:, cols] + term
-            return 0
-
-        lax.fori_loop(0, 4, step, 0)
+        if o < 3:
+            @pl.when(is_first)
+            def _():
+                start(to_relay(o))
+
+        local(dq_s.at[:, pair_rows(o)], dq_hbm.at[0, :, pair_rows(o)], osem.at[0, o]).start()
 
     def rebuild(n):
         cols = pl.ds(n * wide, wide)
-        total = acc[:, cols] + branch_term(3, cols)
-        st_s[:, cols] = (st_s[:, cols].astype(jnp.float32) - total).astype(jnp.bfloat16)
+
+        def step(o, _):
+            pair = lax.rem(x + o + o // 2 - 2 * (o // 3), 4)
+            heads = pl.ds(pl.multiple_of(pair * pw, pw), pw)
+            left = jnp.concatenate([att[r, o] for r in range(4)], axis=1)
+            term = dot(left, w_s[:, heads, cols].reshape(4 * pw, wide))
+
+            @pl.when(o == 0)
+            def _():
+                acc[...] = term
+
+            @pl.when(o > 0)
+            def _():
+                acc[...] += term
+
+            return 0
+
+        lax.fori_loop(0, PAIRS, step, 0)
+        st_s[:, cols] = (st_s[:, cols].astype(jnp.float32) - acc[...]).astype(jnp.bfloat16)
+        stream_on(n).start()
 
     def att_relay(o):
         arrive(att_own(o))
@@ -314,15 +375,23 @@
     for key in ("k", "v", "q", "w", "g", "s"):
         loads[key].start()
 
-    pl.semaphore_wait(barrier, len(partners))
-    w_first(RIGHT).start()
-    w_first(LEFT).start()
+    awaited = len(partners) + jnp.where(is_first, 3, 0) + jnp.where(is_relay, 1, 0)
+    pl.semaphore_wait(barrier, awaited)
+    for f in range(2):
+        w_first(RIGHT, f).start()
+        w_first(LEFT, f).start()
 
     @pl.when(has_next)
     def _():
         start(halo())
 
-    w_first(FAR).start()
+    for f in range(2):
+        w_first(FAR, f).start()
+
+    @pl.when(x > 0)
+    def _():
+        for s in range(4):
+            grad_on(s).start()
 
     @pl.when(jnp.logical_not(has_prev))
     def _():
@@ -334,105 +403,116 @@
         ret_in[...] = jnp.zeros(ret_in.shape, ret_in.dtype)
 
     fill_bias()
+    for f in range(2):
+        own_block(LEFT, f)
+        own_block(RIGHT, f)
     for key in ("k", "v", "q"):
         loads[key].wait()
-    own_block(LEFT)
-    own_block(RIGHT)
-    own_block(FAR)
+    own_block(FAR, 0)
+    up_block(LEFT, 0)
+    up_block(RIGHT, 0)
 
     @pl.when(has_prev)
     def _():
         arrive(halo())
 
-    for s in range(4):
-        grad_on(s).start()
+    @pl.when(x == 0)
+    def _():
+        for s in range(4):
+            grad_on(s).start()
+
     forward(0)
     start(att_own(0))
-    up_block(LEFT)
+    own_block(FAR, 1)
+    up_block(LEFT, 1)
+    up_block(RIGHT, 1)
+    forward(1)
+    start(att_own(1))
+    att_relay(0)
+    up_block(FAR, 0)
+    down_block(LEFT, 0)
+    down_block(RIGHT, 0)
+    forward(2)
+    start(att_own(2))
+    att_relay(1)
+    up_block(FAR, 1)
+    forward(3)
+    start(att_own(3))
+    att_relay(2)
+    down_block(LEFT, 1)
     loads["w"].wait()
     loads["g"].wait()
     mate_blocks(0)
     d_out_terms(0)
     start(far_terms(0))
     start(plain_terms(0))
-    forward(1)
-    start(att_own(1))
-    att_relay(0)
-    merge(0)
-    up_block(RIGHT)
-    down_block(LEFT)
-    forward(2)
-    start(att_own(2))
-    att_relay(1)
-    forward(3)
-    start(att_own(3))
-    att_relay(2)
-    d_out_done(0)
-    down_block(RIGHT)
-    up_block(FAR)
-    arrive(att_pass(0))
-    branch(0)
     att_relay(3)
+    down_block(RIGHT, 1)
+    down_block(FAR, 0)
+    far_block(LEFT, 0)
     mate_blocks(1)
     d_out_terms(1)
     start(far_terms(1))
     start(plain_terms(1))
-    backward(0)
-    merge(1)
-    far_block(LEFT)
-    down_block(FAR)
-    arrive(att_pass(1))
-    branch(1)
+    far_block(RIGHT, 0)
+    down_block(FAR, 1)
+    far_block(FAR, 0)
+    loads["s"].wait()
+    for o in range(PAIRS):
+        arrive(att_pass(o))
     mate_blocks(2)
+    mate_blocks(3, (0,))
+    rebuild(0)
+    rebuild(1)
+    merge(0)
+    far_block(LEFT, 1)
     d_out_terms(2)
     start(far_terms(2))
     start(plain_terms(2))
-    arrive(att_pass(2))
-    branch(2)
-    far_block(RIGHT)
-    far_block(FAR)
-    arrive(att_pass(3))
-    loads["s"].wait()
-    mate_blocks(3)
-    for n in range(4):
-        rebuild(n)
-        stream_on(n).start()
+    far_block(RIGHT, 1)
+    far_block(FAR, 1)
+    merge(1)
+    mate_blocks(3, (1,))
     d_out_terms(3)
     start(far_terms(3))
     start(plain_terms(3))
+    rebuild(2)
+    d_out_done(0)
     merge(2)
+    backward(0)
+    rebuild(3)
     d_out_done(1)
+    merge(3)
     backward(1)
-    merge(3)
     d_out_done(2)
     backward(2)
+    relay_on(0)
+    relay_on(1)
     d_out_done(3)
     backward(3)
-
-    out_q = local(dq_s, dq_hbm.at[0], osem.at[0])
-    out_q.start()
-    outs = [out_q]
-
-    @pl.when(has_next)
-    def _():
-        for p in range(PAIRS):
+    relay_on(2)
+
+    chip_next = lax.rem(x + core, 4)
+    pairs_next = [lax.rem(chip_next + n, 4) for n in (0, 1, 3, 2)]
+    for o, p in enumerate(pairs_next):
+        @pl.when(has_next)
+        def _():
             arrive(back(p))
 
-    for i, (ref, out) in enumerate(((k_s, dk_hbm), (v_s, dv_hbm))):
-        here = ref.at[pl.ds(rows, rows)]
-        for o in range(PAIRS):
-            total = mine[i, o] + ret_in[i, xs[o]].astype(jnp.float32)
-            ref[pl.ds(rows, rows), pair_rows(o)] = total.astype(jnp.bfloat16)
-        outs.append(local(here, out.at[0], osem.at[1 + i]))
-        outs[-1].start()
+        cols = pl.ds(pl.multiple_of(p * pw, pw), pw)
+        for i, (ref, out) in enumerate(((k_s, dk_hbm), (v_s, dv_hbm))):
+            total = mine[i, p] + ret_in[i, p].astype(jnp.float32)
+            ref[pl.ds(rows, rows), cols] = total.astype(jnp.bfloat16)
+            local(ref.at[pl.ds(rows, rows), cols], out.at[0, :, cols], osem.at[1 + i, o]).start()
 
     for r in (LEFT, RIGHT, FAR):
-        w_first((4 - r) % 4).wait_send()
-        w_up(r, x).wait_send()
-        w_down(r, x).wait_send()
-        w_far(r, xs[1] if r != FAR else xs[2]).wait_send()
-        for o in range(PAIRS):
-            w_mate(r, o, core).wait_send()
+        for f in range(2):
+            w_first((4 - r) % 4, f).wait_send()
+            w_up(r, f, x).wait_send()
+            w_down(r, f, x).wait_send()
+            w_far(r, f, xs[2] if (r, f) in upward else xs[1]).wait_send()
+            for o in range(PAIRS):
+                w_mate(r, f, o, core).wait_send()
     for o in range(PAIRS):
         sent(att_own(o))
         sent(att_pass(o))
@@ -450,11 +530,27 @@
 
     @pl.when(has_prev)
     def _():
-        for p in range(PAIRS):
-            sent(back(p))
-
-    for copy in outs:
-        copy.wait()
+        sent(back(xs[3]))
+
+    @pl.when(has_prev & jnp.logical_not(is_first))
+    def _():
+        for o in range(3):
+            sent(back(xs[o]))
+
+    @pl.when(is_first)
+    def _():
+        for o in range(3):
+            sent(to_relay(o))
+
+    @pl.when(is_relay)
+    def _():
+        sent(from_relay())
+
+    for o, p in enumerate(pairs_next):
+        local(dq_s.at[:, pair_rows(o)], dq_hbm.at[0, :, pair_rows(o)], osem.at[0, o]).wait()
+        cols = pl.ds(pl.multiple_of(p * pw, pw), pw)
+        for i, (ref, out) in enumerate(((k_s, dk_hbm), (v_s, dv_hbm))):
+            local(ref.at[pl.ds(rows, rows), cols], out.at[0, :, cols], osem.at[1 + i, o]).wait()
 
 
 def body(queries, keys, values, stream, grad_stream, out_proj, doc_ids):
@@ -484,19 +580,20 @@
             pltpu.VMEM((PAIRS, pw, rows), bf),
             pltpu.VMEM((8, 2, 3 * qb, qb), bf),
             pltpu.VMEM((2, 3 * qb, qb), f32),
-            pltpu.VMEM((rows, shard), f32),
+            pltpu.VMEM((rows, shard // 4), f32),
             pltpu.VMEM((2, PAIRS, rows, pw), bf),
             pltpu.VMEM((2, PAIRS, rows, pw), bf),
+            pltpu.VMEM((2, rows, pw), bf),
             pltpu.VMEM((2, PAIRS, rows, pw), f32),
             pltpu.VMEM((rows, width), bf),
             pltpu.VMEM((PAIRS, pw, qb), bf),
             pltpu.VMEM((PAIRS, pw, qb), bf),
             pltpu.VMEM((PAIRS, pw, rows), bf),
             pltpu.VMEM((PAIRS, pw, rows), bf),
-            dma((6,)), dma((3,)),
-            dma((3,)), dma((3,)), dma((3, 3)), dma((3, 3)), dma((4, 3)), dma((4, 3)),
+            dma((6,)), dma((3, 4)),
+            dma((3, 2)), dma((3, 2)), dma((3, 3, 2)), dma((3, 3, 2)), dma((4, 3, 2)), dma((4, 3, 2)),
             dma((4, 4)), dma((4, 4)),
-            dma((2,)), dma((2,)), dma((2, 4)), dma((2, 4)),
+            dma((2,)), dma((2,)), dma((2, 5)), dma((2, 4)), dma((2, 3)), dma((2,)),
             dma((3, 2, 4)), dma((3, 2, 4)),
             dma((4,)), dma((4,)), dma((4,)), dma((4,)),
         ],

time: 169 us -> 154 us (0.911)
  the two profiles are of different devices: /device:TPU:22 before, /device:TPU:39 now
where the time goes in v3:
time: 154 us
  Pallas kernels  145 us (94%)
  local copies, waits for them, and re-layouts  8.1 us (5%)
    pallas_call x1, Pallas kernels, body(): pl.pallas_call(functools.partial(kernel, rows, width, shard, *sizes), out...  145 us
    unnamed x13, local copies, waits for them, and re-layouts  8.1 us

profile of v3, /device:TPU:39, one launch (start us, length us, event | category | flops | bytes accessed | tf_op | source)
XLA Modules:
  0.0 153.6 jit_solution(9458734525970642849)
XLA Ops:
  0.6 144.8 %shard_map.110 = (bf16[1,512,1024]{2,1,0:T(8,128)(2,1)}, bf16[1,512,1024]{2,1,0:T(8,128)(2,1)}, bf16[1,512,1024]{2,1,0:T(8,128)(2,1)}, bf16[1,512,2048]{2,1,0:T(8,128)(2,1)}, bf16[1,512,2048]{2,1,0:T(8,128)(2,1)}) custom-call(bf16[1,512,1024]{2,1,0:T(8,128)(2,1)} %q_hbm.1, bf16[1,512,1024]{2,1,0:T(8,128)(2,1)} %k_hbm.1, bf16[1,512,1024]{2,1,0:T(8,128)(2,1)} %v_hbm.1, ...), custom_call_target="tpu_custom_call" | custom-call | tf_op jit(solution)/shard_map/pallas_call | solution.py:566
  145.5 0.0 copy-start.3
  145.5 0.0 copy-start.2
  145.5 2.4 %copy.17 = bf16[1,512,1024]{2,1,0:T(8,128)(2,1)} copy(bf16[1,512,1024]{2,1,0:T(8,128)(2,1)} %get-tuple-element.10) | data formatting | bytes 2097152
  147.9 0.0 copy-done.3
  147.9 0.0 copy-start.1
  147.9 1.0 copy.18
  148.9 0.0 copy-done.2
  148.9 1.0 copy.19
  149.9 0.1 copy-done.1
  149.9 0.0 copy-start
  149.9 1.3 copy.20
  151.2 1.0 copy-done
  152.3 1.3 copy.21
Async XLA Ops:
  145.5 2.4 %copy-start.3 = (bf16[1,512,1024]{2,1,0:T(8,128)(2,1)S(1)}, bf16[1,512,1024]{2,1,0:T(8,128)(2,1)}, u32[]{:S(2)}) copy-start(bf16[1,512,1024]{2,1,0:T(8,128)(2,1)} %get-tuple-element.11) | copy-start | bytes 3145732
  145.5 3.4 %copy-start.2 = (bf16[1,512,1024]{2,1,0:T(8,128)(2,1)S(1)}, bf16[1,512,1024]{2,1,0:T(8,128)(2,1)}, u32[]{:S(2)}) copy-start(bf16[1,512,1024]{2,1,0:T(8,128)(2,1)} %get-tuple-element.12) | copy-start | bytes 3145732
  147.9 2.0 %copy-start.1 = (bf16[1,512,2048]{2,1,0:T(8,128)(2,1)S(1)}, bf16[1,512,2048]{2,1,0:T(8,128)(2,1)}, u32[]{:S(2)}) copy-start(bf16[1,512,2048]{2,1,0:T(8,128)(2,1)} %get-tuple-element.13) | copy-start | bytes 6291460
  149.9 2.3 %copy-start = (bf16[1,512,2048]{2,1,0:T(8,128)(2,1)S(1)}, bf16[1,512,2048]{2,1,0:T(8,128)(2,1)}, u32[]{:S(2)}) copy-start(bf16[1,512,2048]{2,1,0:T(8,128)(2,1)} %get-tuple-element.14) | copy-start | bytes 6291460

commit v4 on v3

--- a/solution.py
+++ b/solution.py
@@ -129,7 +129,16 @@
 
     def own_block(r, f):
         w_first((4 - r) % 4, f).wait_recv()
-        w_up(r, f, x).start()
+        own_block_on(r, f)
+
+    def own_block_on(r, f):
+        if r == FAR or f == 1:
+            w_up(r, f, x).start()
+        else:
+            @pl.when(core == 1)
+            def _():
+                w_up(r, f, x).start()
+
         w_down(r, f, x).start()
         w_mate(r, f, 0, core).start()
 
@@ -403,12 +412,18 @@
         ret_in[...] = jnp.zeros(ret_in.shape, ret_in.dtype)
 
     fill_bias()
-    for f in range(2):
-        own_block(LEFT, f)
-        own_block(RIGHT, f)
+    own_block(LEFT, 0)
+    own_block(RIGHT, 0)
     for key in ("k", "v", "q"):
         loads[key].wait()
-    own_block(FAR, 0)
+    w_first(FAR, 0).wait_recv()
+
+    @pl.when(core == 0)
+    def _():
+        w_up(LEFT, 0, x).start()
+        w_up(RIGHT, 0, x).start()
+
+    own_block_on(FAR, 0)
     up_block(LEFT, 0)
     up_block(RIGHT, 0)
 
@@ -423,23 +438,24 @@
 
     forward(0)
     start(att_own(0))
+    up_block(FAR, 0)
+    own_block(LEFT, 1)
+    own_block(RIGHT, 1)
     own_block(FAR, 1)
-    up_block(LEFT, 1)
-    up_block(RIGHT, 1)
     forward(1)
     start(att_own(1))
+    down_block(LEFT, 0)
     att_relay(0)
-    up_block(FAR, 0)
-    down_block(LEFT, 0)
-    down_block(RIGHT, 0)
     forward(2)
     start(att_own(2))
+    down_block(RIGHT, 0)
     att_relay(1)
-    up_block(FAR, 1)
     forward(3)
     start(att_own(3))
+    down_block(FAR, 0)
+    far_block(LEFT, 0)
+    far_block(RIGHT, 0)
     att_relay(2)
-    down_block(LEFT, 1)
     loads["w"].wait()
     loads["g"].wait()
     mate_blocks(0)
@@ -447,35 +463,37 @@
     start(far_terms(0))
     start(plain_terms(0))
     att_relay(3)
+    up_block(LEFT, 1)
+    far_block(FAR, 0)
+    down_block(LEFT, 1)
+    up_block(RIGHT, 1)
     down_block(RIGHT, 1)
-    down_block(FAR, 0)
-    far_block(LEFT, 0)
-    mate_blocks(1)
+    loads["s"].wait()
+    for o in range(1, PAIRS):
+        mate_blocks(o, (0,))
+    up_block(FAR, 1)
+    for o in range(PAIRS):
+        arrive(att_pass(o))
+    rebuild(0)
+    down_block(FAR, 1)
+    mate_blocks(1, (1,))
     d_out_terms(1)
     start(far_terms(1))
     start(plain_terms(1))
-    far_block(RIGHT, 0)
-    down_block(FAR, 1)
-    far_block(FAR, 0)
-    loads["s"].wait()
-    for o in range(PAIRS):
-        arrive(att_pass(o))
-    mate_blocks(2)
-    mate_blocks(3, (0,))
-    rebuild(0)
-    rebuild(1)
-    merge(0)
     far_block(LEFT, 1)
+    mate_blocks(2, (1,))
     d_out_terms(2)
     start(far_terms(2))
     start(plain_terms(2))
+    rebuild(1)
     far_block(RIGHT, 1)
     far_block(FAR, 1)
-    merge(1)
+    merge(0)
     mate_blocks(3, (1,))
     d_out_terms(3)
     start(far_terms(3))
     start(plain_terms(3))
+    merge(1)
     rebuild(2)
     d_out_done(0)
     merge(2)

time: 154 us -> 142 us (0.922)
  the two profiles are of different devices: /device:TPU:39 before, /device:TPU:1 now
where the time goes in v4:
time: 142 us
  Pallas kernels  133 us (94%)
  local copies, waits for them, and re-layouts  8.1 us (6%)
    pallas_call x1, Pallas kernels, body(): pl.pallas_call(functools.partial(kernel, rows, width, shard, *sizes), out...  133 us
    unnamed x13, local copies, waits for them, and re-layouts  8.1 us

profile of v4, /device:TPU:1, one launch (start us, length us, event | category | flops | bytes accessed | tf_op | source)
XLA Modules:
  0.0 141.8 jit_solution(529976662297264346)
XLA Ops:
  0.6 133.1 %shard_map.110 = (bf16[1,512,1024]{2,1,0:T(8,128)(2,1)}, bf16[1,512,1024]{2,1,0:T(8,128)(2,1)}, bf16[1,512,1024]{2,1,0:T(8,128)(2,1)}, bf16[1,512,2048]{2,1,0:T(8,128)(2,1)}, bf16[1,512,2048]{2,1,0:T(8,128)(2,1)}) custom-call(bf16[1,512,1024]{2,1,0:T(8,128)(2,1)} %q_hbm.1, bf16[1,512,1024]{2,1,0:T(8,128)(2,1)} %k_hbm.1, bf16[1,512,1024]{2,1,0:T(8,128)(2,1)} %v_hbm.1, ...), custom_call_target="tpu_custom_call" | custom-call | tf_op jit(solution)/shard_map/pallas_call | solution.py:584
  133.7 0.0 copy-start.3
  133.7 0.0 copy-start.2
  133.7 2.4 %copy.17 = bf16[1,512,1024]{2,1,0:T(8,128)(2,1)} copy(bf16[1,512,1024]{2,1,0:T(8,128)(2,1)} %get-tuple-element.10) | data formatting | bytes 2097152
  136.1 0.0 copy-done.3
  136.1 0.0 copy-start.1
  136.1 1.0 copy.18
  137.1 0.0 copy-done.2
  137.1 1.0 copy.19
  138.1 0.1 copy-done.1
  138.2 0.0 copy-start
  138.2 1.3 copy.20
  139.5 1.0 copy-done
  140.5 1.3 copy.21
Async XLA Ops:
  133.7 2.4 %copy-start.3 = (bf16[1,512,1024]{2,1,0:T(8,128)(2,1)S(1)}, bf16[1,512,1024]{2,1,0:T(8,128)(2,1)}, u32[]{:S(2)}) copy-start(bf16[1,512,1024]{2,1,0:T(8,128)(2,1)} %get-tuple-element.11) | copy-start | bytes 3145732
  133.7 3.4 %copy-start.2 = (bf16[1,512,1024]{2,1,0:T(8,128)(2,1)S(1)}, bf16[1,512,1024]{2,1,0:T(8,128)(2,1)}, u32[]{:S(2)}) copy-start(bf16[1,512,1024]{2,1,0:T(8,128)(2,1)} %get-tuple-element.12) | copy-start | bytes 3145732
  136.1 2.0 %copy-start.1 = (bf16[1,512,2048]{2,1,0:T(8,128)(2,1)S(1)}, bf16[1,512,2048]{2,1,0:T(8,128)(2,1)}, u32[]{:S(2)}) copy-start(bf16[1,512,2048]{2,1,0:T(8,128)(2,1)} %get-tuple-element.13) | copy-start | bytes 6291460
  138.2 2.3 %copy-start = (bf16[1,512,2048]{2,1,0:T(8,128)(2,1)S(1)}, bf16[1,512,2048]{2,1,0:T(8,128)(2,1)}, u32[]{:S(2)}) copy-start(bf16[1,512,2048]{2,1,0:T(8,128)(2,1)} %get-tuple-element.14) | copy-start | bytes 6291460

commit v5 on v4

--- a/solution.py
+++ b/solution.py
@@ -472,42 +472,42 @@
     for o in range(1, PAIRS):
         mate_blocks(o, (0,))
     up_block(FAR, 1)
+    mate_blocks(1, (1,))
+    d_out_terms(1)
+    start(far_terms(1))
+    start(plain_terms(1))
     for o in range(PAIRS):
         arrive(att_pass(o))
     rebuild(0)
     down_block(FAR, 1)
-    mate_blocks(1, (1,))
-    d_out_terms(1)
-    start(far_terms(1))
-    start(plain_terms(1))
-    far_block(LEFT, 1)
+    merge(0)
     mate_blocks(2, (1,))
     d_out_terms(2)
     start(far_terms(2))
     start(plain_terms(2))
+    far_block(LEFT, 1)
     rebuild(1)
     far_block(RIGHT, 1)
     far_block(FAR, 1)
-    merge(0)
     mate_blocks(3, (1,))
     d_out_terms(3)
     start(far_terms(3))
     start(plain_terms(3))
     merge(1)
+    d_out_done(0)
+    backward(0)
+    merge(2)
     rebuild(2)
-    d_out_done(0)
-    merge(2)
-    backward(0)
+    d_out_done(1)
+    backward(1)
+    merge(3)
     rebuild(3)
-    d_out_done(1)
-    merge(3)
-    backward(1)
     d_out_done(2)
     backward(2)
     relay_on(0)
-    relay_on(1)
     d_out_done(3)
     backward(3)
+    relay_on(1)
     relay_on(2)
 
     chip_next = lax.rem(x + core, 4)

time: 142 us -> 140 us (0.986)
  the two profiles are of different devices: /device:TPU:1 before, /device:TPU:22 now
where the time goes in v5:
time: 140 us; the launch traced here: 138 us
  Pallas kernels  129 us (92%)
  local copies, waits for them, and re-layouts  8.1 us (6%)
    pallas_call x1, Pallas kernels, body(): pl.pallas_call(functools.partial(kernel, rows, width, shard, *sizes), out...  129 us
    unnamed x13, local copies, waits for them, and re-layouts  8.1 us

profile of v5, /device:TPU:22, one launch (start us, length us, event | category | flops | bytes accessed | tf_op | source)
XLA Modules:
  0.0 138.2 jit_solution(5424166505122745441)
XLA Ops:
  0.6 129.4 %shard_map.110 = (bf16[1,512,1024]{2,1,0:T(8,128)(2,1)}, bf16[1,512,1024]{2,1,0:T(8,128)(2,1)}, bf16[1,512,1024]{2,1,0:T(8,128)(2,1)}, bf16[1,512,2048]{2,1,0:T(8,128)(2,1)}, bf16[1,512,2048]{2,1,0:T(8,128)(2,1)}) custom-call(bf16[1,512,1024]{2,1,0:T(8,128)(2,1)} %q_hbm.1, bf16[1,512,1024]{2,1,0:T(8,128)(2,1)} %k_hbm.1, bf16[1,512,1024]{2,1,0:T(8,128)(2,1)} %v_hbm.1, ...), custom_call_target="tpu_custom_call" | custom-call | tf_op jit(solution)/shard_map/pallas_call | solution.py:584
  130.1 0.0 copy-start.3
  130.1 0.0 copy-start.2
  130.1 2.4 %copy.17 = bf16[1,512,1024]{2,1,0:T(8,128)(2,1)} copy(bf16[1,512,1024]{2,1,0:T(8,128)(2,1)} %get-tuple-element.10) | data formatting | bytes 2097152
  132.5 0.0 copy-done.3
  132.5 0.0 copy-start.1
  132.5 1.0 copy.18
  133.5 0.0 copy-done.2
  133.5 1.0 copy.19
  134.4 0.1 copy-done.1
  134.5 0.0 copy-start
  134.5 1.3 copy.20
  135.8 1.0 copy-done
  136.9 1.3 copy.21
Async XLA Ops:
  130.1 2.4 %copy-start.3 = (bf16[1,512,1024]{2,1,0:T(8,128)(2,1)S(1)}, bf16[1,512,1024]{2,1,0:T(8,128)(2,1)}, u32[]{:S(2)}) copy-start(bf16[1,512,1024]{2,1,0:T(8,128)(2,1)} %get-tuple-element.11) | copy-start | bytes 3145732
  130.1 3.4 %copy-start.2 = (bf16[1,512,1024]{2,1,0:T(8,128)(2,1)S(1)}, bf16[1,512,1024]{2,1,0:T(8,128)(2,1)}, u32[]{:S(2)}) copy-start(bf16[1,512,1024]{2,1,0:T(8,128)(2,1)} %get-tuple-element.12) | copy-start | bytes 3145732
  132.5 2.0 %copy-start.1 = (bf16[1,512,2048]{2,1,0:T(8,128)(2,1)S(1)}, bf16[1,512,2048]{2,1,0:T(8,128)(2,1)}, u32[]{:S(2)}) copy-start(bf16[1,512,2048]{2,1,0:T(8,128)(2,1)} %get-tuple-element.13) | copy-start | bytes 6291460
  134.5 2.3 %copy-start = (bf16[1,512,2048]{2,1,0:T(8,128)(2,1)S(1)}, bf16[1,512,2048]{2,1,0:T(8,128)(2,1)}, u32[]{:S(2)}) copy-start(bf16[1,512,2048]{2,1,0:T(8,128)(2,1)} %get-tuple-element.14) | copy-start | bytes 6291460

commit v6 on v5

--- a/solution.py
+++ b/solution.py
@@ -233,7 +233,7 @@
         here = pl.ds(s * sub, sub)
         return remote(g_hbm.at[0, here], ng_hbm.at[0, here], pgs.at[s], pgr.at[s], {"pipe": other})
 
-    wide = shard // 4
+    wide = shard // 8
 
     def stream_on(n):
         cols = pl.ds(n * wide, wide)
@@ -355,6 +355,10 @@
         local(dq_s.at[:, pair_rows(o)], dq_hbm.at[0, :, pair_rows(o)], osem.at[0, o]).start()
 
     def rebuild(n):
+        rebuild_part(2 * n)
+        rebuild_part(2 * n + 1)
+
+    def rebuild_part(n):
         cols = pl.ds(n * wide, wide)
 
         def step(o, _):
@@ -505,9 +509,9 @@
     d_out_done(2)
     backward(2)
     relay_on(0)
+    relay_on(1)
     d_out_done(3)
     backward(3)
-    relay_on(1)
     relay_on(2)
 
     chip_next = lax.rem(x + core, 4)
@@ -539,8 +543,9 @@
         sent(merged_terms(o))
         grad_on(o).wait_send()
         grad_on(o).wait_recv()
-        stream_on(o).wait_send()
-        stream_on(o).wait_recv()
+        for n in (2 * o, 2 * o + 1):
+            stream_on(n).wait_send()
+            stream_on(n).wait_recv()
 
     @pl.when(has_next)
     def _():
@@ -598,7 +603,7 @@
             pltpu.VMEM((PAIRS, pw, rows), bf),
             pltpu.VMEM((8, 2, 3 * qb, qb), bf),
             pltpu.VMEM((2, 3 * qb, qb), f32),
-            pltpu.VMEM((rows, shard // 4), f32),
+            pltpu.VMEM((rows, shard // 8), f32),
             pltpu.VMEM((2, PAIRS, rows, pw), bf),
             pltpu.VMEM((2, PAIRS, rows, pw), bf),
             pltpu.VMEM((2, rows, pw), bf),
@@ -613,7 +618,7 @@
             dma((4, 4)), dma((4, 4)),
             dma((2,)), dma((2,)), dma((2, 5)), dma((2, 4)), dma((2, 3)), dma((2,)),
             dma((3, 2, 4)), dma((3, 2, 4)),
-            dma((4,)), dma((4,)), dma((4,)), dma((4,)),
+            dma((4,)), dma((4,)), dma((8,)), dma((8,)),
         ],
         compiler_params=pltpu.CompilerParams(
             collective_id=0, has_side_effects=True, vmem_limit_bytes=67043328

time: 140 us -> 142 us (1.014)
  the two profiles are of different devices: /device:TPU:22 before, /device:TPU:1 now
where the time goes in v6:
time: 142 us; the launch traced here: 141 us
  Pallas kernels  133 us (94%)
  local copies, waits for them, and re-layouts  8.1 us (6%)
    pallas_call x1, Pallas kernels, body(): pl.pallas_call(functools.partial(kernel, rows, width, shard, *sizes), out...  133 us
    unnamed x13, local copies, waits for them, and re-layouts  8.1 us

profile of v6, /device:TPU:1, one launch (start us, length us, event | category | flops | bytes accessed | tf_op | source)
XLA Modules:
  0.0 141.4 jit_solution(11623150376982784402)
XLA Ops:
  0.6 132.7 %shard_map.110 = (bf16[1,512,1024]{2,1,0:T(8,128)(2,1)}, bf16[1,512,1024]{2,1,0:T(8,128)(2,1)}, bf16[1,512,1024]{2,1,0:T(8,128)(2,1)}, bf16[1,512,2048]{2,1,0:T(8,128)(2,1)}, bf16[1,512,2048]{2,1,0:T(8,128)(2,1)}) custom-call(bf16[1,512,1024]{2,1,0:T(8,128)(2,1)} %q_hbm.1, bf16[1,512,1024]{2,1,0:T(8,128)(2,1)} %k_hbm.1, bf16[1,512,1024]{2,1,0:T(8,128)(2,1)} %v_hbm.1, ...), custom_call_target="tpu_custom_call" | custom-call | tf_op jit(solution)/shard_map/pallas_call | solution.py:589
  133.3 0.0 copy-start.3
  133.3 0.0 copy-start.2
  133.3 2.4 %copy.17 = bf16[1,512,1024]{2,1,0:T(8,128)(2,1)} copy(bf16[1,512,1024]{2,1,0:T(8,128)(2,1)} %get-tuple-element.10) | data formatting | bytes 2097152
  135.7 0.0 copy-done.3
  135.7 0.0 copy-start.1
  135.7 1.0 copy.18
  136.7 0.0 copy-done.2
  136.7 1.0 copy.19
  137.7 0.1 copy-done.1
  137.7 0.0 copy-start
  137.8 1.3 copy.20
  139.1 1.0 copy-done
  140.1 1.3 copy.21
Async XLA Ops:
  133.3 2.4 %copy-start.3 = (bf16[1,512,1024]{2,1,0:T(8,128)(2,1)S(1)}, bf16[1,512,1024]{2,1,0:T(8,128)(2,1)}, u32[]{:S(2)}) copy-start(bf16[1,512,1024]{2,1,0:T(8,128)(2,1)} %get-tuple-element.11) | copy-start | bytes 3145732
  133.3 3.4 %copy-start.2 = (bf16[1,512,1024]{2,1,0:T(8,128)(2,1)S(1)}, bf16[1,512,1024]{2,1,0:T(8,128)(2,1)}, u32[]{:S(2)}) copy-start(bf16[1,512,1024]{2,1,0:T(8,128)(2,1)} %get-tuple-element.12) | copy-start | bytes 3145732
  135.7 2.0 %copy-start.1 = (bf16[1,512,2048]{2,1,0:T(8,128)(2,1)S(1)}, bf16[1,512,2048]{2,1,0:T(8,128)(2,1)}, u32[]{:S(2)}) copy-start(bf16[1,512,2048]{2,1,0:T(8,128)(2,1)} %get-tuple-element.13) | copy-start | bytes 6291460
  137.7 2.3 %copy-start = (bf16[1,512,2048]{2,1,0:T(8,128)(2,1)S(1)}, bf16[1,512,2048]{2,1,0:T(8,128)(2,1)}, u32[]{:S(2)}) copy-start(bf16[1,512,2048]{2,1,0:T(8,128)(2,1)} %get-tuple-element.14) | copy-start | bytes 6291460
